TPU v7x, 1024 devices: a whole 4x4x32 slice. The times are simulated.
1024 devices in a mesh: ep: 32 (over z), hd: 4 (over x), rep: 8 (over y, core).
Axes of the slice: x: 4, y: 4, z: 32, core: 2. Of those that a mesh axis runs over, the one named last changes fastest.
Arguments:
- queries: bfloat16 [1024, 64, 576], P('ep', ('hd', 'rep')), may hold values from -256 to 256
- latent_cache: bfloat16 [1024, 64, 576], P('ep'), may hold values from -6 to 6
- cached_lengths: int32 [1024], P('ep'), may hold values from 1 to 64
- prefill_rows: bfloat16 [1024, 64, 576], P('ep'), may hold values from -6 to 6
- owner_rank: int32 [1024], P('ep'), may hold values from 0 to 31, as said below
- value_up: bfloat16 [64, 512, 128], P(('hd', 'rep')), may hold values from -1 to 1
- out_proj: bfloat16 [8192, 7168], P(('hd', 'rep')), may hold values from -0.125 to 0.125
Outputs:
- mixed: bfloat16 [1024, 7168], P('ep', ('hd', 'rep'))
- fresh: bfloat16 [1024, 64, 576], P('ep', ('hd', 'rep'))
Inputs may be any that keep to these rules, and one draw needn't show every extreme that they name: `owner_rank`: the 32 requests of one prefill block go to 32 different decode indices.
All inputs are finite; a program needn't handle non-finite values.
Results may differ from a plain program's by a relative error of at most 0.011.
Values may be sent and summed in bfloat16 or wider, within the bound.
No kernel may reach another device: no remote copies, remote signals or barrier semaphores. Data moves between devices by JAX's collectives and lax.ppermute only.
A program may use at most 64 MiB of HBM per device.

v0:
```python
import jax
import jax.numpy as jnp
from jax import lax
from jax.sharding import PartitionSpec as P

LAT = 512


score_scale = 192.0 ** (-0.5)
neg_fill = -1e30


def sent_together(arrays, axis, split_dim, concat_dim, along):
    columns = [a.reshape(*a.shape[:along], -1) for a in arrays]
    both = jnp.concatenate(columns, axis=along)
    out, at, finished = (
        lax.all_to_all(both, axis, split_axis=split_dim, concat_axis=concat_dim, tiled=True),
        0,
        [],
    )
    for a, column in zip(arrays, columns):
        share = out[..., at : at + column.shape[along]]
        finished.append(share.reshape(*share.shape[:along], *a.shape[along:]))
        at += column.shape[along]
    return tuple(finished)


def in_blocks(value, dim, size):
    before, after = (value.shape[:dim], value.shape[dim + 1 :])
    return jnp.moveaxis(value.reshape(*before, size, -1, *after), dim, 0)


def sent_and_summed(value, axis, dim):
    parts = in_blocks(value, dim, lax.axis_size(axis))
    arrived = lax.all_to_all(parts, axis, split_axis=0, concat_axis=0, tiled=True)
    return arrived.sum(axis=0)


def partial_softmax(query_block, keys_all, visible):
    scores = (
        jnp.einsum("rhk,rck->rhc", query_block, keys_all, preferred_element_type=jnp.float32)
        * score_scale
    )
    scores = jnp.where(visible[:, None, :], scores, neg_fill)
    maxima = jnp.max(scores, axis=-1)
    weights = jnp.exp(scores - maxima[..., None])
    totals = jnp.sum(weights, axis=-1)
    summed = jnp.einsum(
        "rhc,rcl->rhl", weights, keys_all[:, :, :LAT], preferred_element_type=jnp.float32
    )
    return (maxima, totals, summed)


def merge_partials(first, second):
    first_max, first_total, first_sum = first
    second_max, second_total, second_sum = second
    maxima = jnp.maximum(first_max, second_max)
    first_scale = jnp.exp(first_max - maxima)
    second_scale = jnp.exp(second_max - maxima)
    totals = first_total * first_scale + second_total * second_scale
    summed = first_sum * first_scale[..., None] + second_sum * second_scale[..., None]
    return (maxima, totals, summed)


def order_rows(choose, rows):
    flattened = rows.reshape(rows.shape[0], -1)
    ordered = jnp.dot(choose, flattened, preferred_element_type=jnp.float32).astype(jnp.bfloat16)
    return ordered.reshape(rows.shape)


def body(queries, latent_cache, cached_lengths, prefill_rows, owner_rank, value_up, out_proj):
    count = latent_cache.shape[0]
    context = latent_cache.shape[1]
    fresh_count = prefill_rows.shape[1]
    share = fresh_count // lax.axis_size(("hd", "rep"))
    group = lax.axis_index(("hd", "rep"))
    choose = (owner_rank[None, :] == jnp.arange(count, dtype=jnp.int32)[:, None]).astype(
        jnp.bfloat16
    )
    position = jnp.arange(context, dtype=jnp.int32)
    in_cache = position[None, :] < cached_lengths[:, None]
    own_rows = lax.dynamic_slice_in_dim(prefill_rows, group * share, share, 1)
    ordered = order_rows(choose, own_rows)
    fresh_shard = lax.all_to_all(ordered, "ep", split_axis=0, concat_axis=0, tiled=True)
    incoming = lax.all_to_all(queries, "ep", split_axis=0, concat_axis=0, tiled=True)
    by_source = jnp.einsum(
        "dj,dhk->jhk", choose, incoming, preferred_element_type=jnp.float32
    ).astype(jnp.bfloat16)
    always = jnp.ones((count, fresh_count), dtype=bool)
    far_maxima, far_totals, far_summed = partial_softmax(by_source, prefill_rows, always)
    choose_wide = choose.astype(jnp.float32)
    far_maxima = jnp.dot(choose_wide, far_maxima, precision=lax.Precision.HIGHEST)
    far_totals = jnp.dot(choose_wide, far_totals, precision=lax.Precision.HIGHEST)
    far_summed = jnp.einsum("dj,jhl->dhl", choose_wide, far_summed, precision=lax.Precision.HIGHEST)
    far_part = sent_together((far_maxima, far_totals, far_summed), "ep", 0, 0, 2)
    near = partial_softmax(queries, latent_cache, in_cache)
    maxima, totals, summed = merge_partials(near, far_part)
    latent_out = summed / totals[..., None]
    head_out = jnp.einsum(
        "rhl,hlv->rhv",
        latent_out.astype(jnp.bfloat16),
        value_up,
        preferred_element_type=jnp.float32,
    )
    head_out = head_out.astype(jnp.bfloat16).reshape(count, -1)
    partial_term = jnp.dot(head_out, out_proj, preferred_element_type=jnp.float32)
    mixed = sent_and_summed(partial_term, ("hd", "rep"), 1).astype(jnp.bfloat16)
    return (mixed, fresh_shard)


def solution(mesh):
    in_specs = (
        P("ep", ("hd", "rep"), None),
        P("ep", None, None),
        P("ep"),
        P("ep", None, None),
        P("ep"),
        P(("hd", "rep"), None, None),
        P(("hd", "rep"), None),
    )
    out_specs = (P("ep", ("hd", "rep")), P("ep", ("hd", "rep"), None))
    return jax.shard_map(body, mesh=mesh, in_specs=in_specs, out_specs=out_specs, check_vma=False)
```

profile of v0, /device:TPU:1, one launch (start us, length us, event | category | flops | bytes accessed | tf_op | source)
XLA Modules:
  0.0 154.9 jit_solution(4568924544585562430)
XLA Ops:
  0.7 55.0 %all_to_all.20 = bf16[32,2,576]{2,1,0:T(2,128)(2,1)S(1)} all-to-all(bf16[32,2,576]{2,1,0:T(2,128)(2,1)} %param.7), channel_id=1, replica_groups=mesh['ep'=32,'hd'=4,'rep'=8] {'ep'}, dimensions={0} | all-to-all | bytes 147456 | tf_op jit(solution)/shard_map/all_to_all | solution.py:85
  55.6 0.9 convolution_convert_fusion.1
  56.6 2.8 %fusion.42 = (f32[32,2]{1,0:T(8,128)S(1)}, f32[32,2,64]{2,1,0:T(2,128)S(1)}) fusion(bf16[32,64,576]{2,1,0:T(8,128)(2,1)} %param.10, bf16[32,2,576]{2,0,1:T(8,128)(2,1)S(1)} %convolution_convert_fusion.1), kind=kOutput, calls=%fused_computation.50 | convolution fusion | flops 4726720 | bytes 2449664 | tf_op jit(solution)/shard_map/rhk,rck->rhc/dot_general | solution.py:41
  59.4 0.5 fusion
  59.8 0.2 fusion.24
  60.0 0.2 convolution_bitcast_fusion.2
  60.2 0.2 fusion.18
  60.4 0.2 convolution_bitcast_fusion.1
  60.6 0.1 copy.47
  60.7 0.1 copy.46
  60.8 0.1 pad_maximum_fusion
  60.9 0.8 copy.48
  61.7 3.9 %all-to-all-start.1 = ((f32[32,2,514]{2,1,0:T(2,128)}), f32[32,2,514]{2,1,0:T(2,128)S(1)}, u32[]{:S(2)}, u32[]{:S(2)}) async-start(f32[32,2,514]{2,1,0:T(2,128)} %copy.48), calls=%async_computation.1 | async-start | bytes 327680 | tf_op jit(solution)/shard_map/all_to_all | solution.py:17
  65.7 2.7 %fusion.43 = (f32[32,2]{1,0:T(8,128)S(1)}, f32[32,2,64]{2,1,0:T(2,128)S(1)}) fusion(bf16[32,2,576]{2,1,0:T(2,128)(2,1)S(1)} %copy-done.2, bf16[32,64,576]{2,1,0:T(8,128)(2,1)} %param.8, pred[32,64]{1,0:T(8,128)(4,1)S(1)} %iota_compare_fusion.4), kind=kOutput, calls=%fused_computation.51 | convolution fusion | flops 4730816 | bytes 2451712 | tf_op jit(solution)/shard_map/rhk,rck->rhc/dot_general | solution.py:41
  68.5 0.2 fusion.23
  68.8 5.9 %copy.57 = bf16[256,7168]{0,1:T(8,128)(2,1)} copy(bf16[256,7168]{1,0:T(8,128)(2,1)} %param.13) | data formatting | bytes 7340032 | tf_op args[6]
  74.7 0.1 constant_dynamic-slice_fusion
  74.8 0.1 reshape.50
  74.9 0.1 convolution_convert_fusion
  75.1 0.8 reshape.51
  75.8 20.2 %all-to-all-done.1 = f32[32,2,514]{2,1,0:T(2,128)S(1)} async-done(((f32[32,2,514]{2,1,0:T(2,128)}), f32[32,2,514]{2,1,0:T(2,128)S(1)}, u32[]{:S(2)}, u32[]{:S(2)}) %all-to-all-start.1) | async-done | bytes 131616 | tf_op jit(solution)/shard_map/all_to_all | solution.py:17
  96.0 5.5 %all-to-all-start.3 = ((bf16[32,2,576]{2,1,0:T(2,128)(2,1)}), bf16[32,2,576]{2,1,0:T(2,128)(2,1)S(1)}, u32[]{:S(2)}, u32[]{:S(2)}) async-start(bf16[32,2,576]{2,1,0:T(2,128)(2,1)} %reshape.51), calls=%async_computation.3 | async-start | bytes 163840 | tf_op jit(solution)/shard_map/all_to_all | solution.py:84
  101.5 0.1 fusion.41
  101.6 0.1 copy.60
  101.7 0.1 copy.61
  102.0 2.1 %fusion.13 = bf16[32,2,512]{2,1,0:T(2,128)(2,1)S(1)} fusion(bf16[32,64,576]{2,1,0:T(8,128)(2,1)} %param.8, f32[32,2,514]{2,1,0:T(2,128)S(1)} %all-to-all-done.1, f32[32,2]{1,0:T(8,128)S(1)} %copy.54, f32[32,2]{1,0:T(8,128)S(1)} %copy.51, f32[32,2]{1,0:T(8,128)S(1)} %copy.50, f32[32,2,64]{2,1,0:T(2,128)S(1)} %get-tuple-element.10, ...), kind=kOutput, calls=%fused_computation.10 | convolution fusion | flops 4362240 | bytes 2311168 | tf_op jit(solution)/shard_map/rhc,rcl->rhl/dot_general | solution.py:48
  104.1 0.2 fusion.17
  104.3 3.2 %convolution_bitcast_fusion = f32[32,32,224]{2,1,0:T(8,128)S(1)} fusion(bf16[32,256,1]{1,0,2:T(8,128)(2,1)S(1)} %reshape.54, bf16[32,224,256]{2,1,0:T(8,128)(2,1)} %bitcast.48), kind=kOutput, calls=%fused_computation.5 | convolution fusion | flops 117440512 | bytes 4603904 | tf_op jit(solution)/shard_map/dot_general | solution.py:106
  107.6 17.9 %all-to-all-done.3 = bf16[32,2,576]{2,1,0:T(2,128)(2,1)S(1)} async-done(((bf16[32,2,576]{2,1,0:T(2,128)(2,1)}), bf16[32,2,576]{2,1,0:T(2,128)(2,1)S(1)}, u32[]{:S(2)}, u32[]{:S(2)}) %all-to-all-start.3) | async-done | bytes 73760 | tf_op jit(solution)/shard_map/all_to_all | solution.py:84
  125.5 28.1 %all_to_all.21 = f32[32,32,224]{2,1,0:T(8,128)S(1)} all-to-all(f32[32,32,224]{2,1,0:T(8,128)S(1)} %convolution_bitcast_fusion), channel_id=1, replica_groups=mesh['ep'=32,'hd'=4,'rep'=8] {'hd','rep'}, dimensions={0} | all-to-all | bytes 1835008 | tf_op jit(solution)/shard_map/all_to_all | solution.py:35
  153.6 0.7 reduce_sum.32
  154.3 0.6 copy.73
  (19 shorter events, 0.6 us)
Async XLA Ops:
  0.6 103.5 %copy-start = (bf16[2,512,128]{2,1,0:T(8,128)(2,1)S(1)}, bf16[2,512,128]{2,1,0:T(8,128)(2,1)}, u32[]{:S(2)}) copy-start(bf16[2,512,128]{2,1,0:T(8,128)(2,1)} %param.12) | copy-start | bytes 786436
  0.6 58.7 %copy-start.1 = (bf16[32,64,576]{2,1,0:T(8,128)(2,1)S(1)}, bf16[32,64,576]{2,1,0:T(8,128)(2,1)}, u32[]{:S(2)}) copy-start(bf16[32,64,576]{2,1,0:T(8,128)(2,1)} %param.10) | copy-start | bytes 7077892
  55.6 4.4 %copy-start.3 = (s32[32]{0:T(128)S(1)}, s32[32]{0:T(128)}, u32[]{:S(2)}) copy-start(s32[32]{0:T(128)} %param.11) | copy-start | bytes 388
  56.6 9.0 %copy-start.4 = (s32[32]{0:T(128)S(1)}, s32[32]{0:T(128)}, u32[]{:S(2)}) copy-start(s32[32]{0:T(128)} %param.9) | copy-start | bytes 388
  56.6 9.1 %copy-start.2 = (bf16[32,2,576]{2,1,0:T(2,128)(2,1)S(1)}, bf16[32,2,576]{2,1,0:T(2,128)(2,1)}, u32[]{:S(2)}) copy-start(bf16[32,2,576]{2,1,0:T(2,128)(2,1)} %param.7) | copy-start | bytes 221188
  61.7 34.3 %all-to-all-start.1 = ((f32[32,2,514]{2,1,0:T(2,128)}), f32[32,2,514]{2,1,0:T(2,128)S(1)}, u32[]{:S(2)}, u32[]{:S(2)}) async-start(f32[32,2,514]{2,1,0:T(2,128)} %copy.48), calls=%async_computation.1 | async-start | bytes 327680 | tf_op jit(solution)/shard_map/all_to_all | solution.py:17
  96.0 29.5 %all-to-all-start.3 = ((bf16[32,2,576]{2,1,0:T(2,128)(2,1)}), bf16[32,2,576]{2,1,0:T(2,128)(2,1)S(1)}, u32[]{:S(2)}, u32[]{:S(2)}) async-start(bf16[32,2,576]{2,1,0:T(2,128)(2,1)} %reshape.51), calls=%async_computation.3 | async-start | bytes 163840 | tf_op jit(solution)/shard_map/all_to_all | solution.py:84
where the time goes:
time: 156 us; the launch traced here: 155 us
  blocking collectives  83.1 us (53%)
  waiting for transfers between devices  38.1 us (24%)
  matrix products  13.1 us (8%)
  starting transfers between devices  9.32 us (6%)
  local copies, waits for them, and re-layouts  9.27 us (6%)
    all_to_all x1, blocking collectives, body(): lax.all_to_all(queries, 'ep', split_axis=0, concat_axis=0, tiled=True)  55 us
    all_to_all x1, blocking collectives, sent_and_summed(): lax.all_to_all(parts, axis, split_axis=0, concat_axis=0, tiled=True)  28.1 us
    all_to_all x1, waiting for transfers between devices, sent_together(): lax.all_to_all(both, axis, split_axis=split_dim, concat_axis=concat_dim,...  20.2 us
    all_to_all x1, waiting for transfers between devices, body(): lax.all_to_all(ordered, 'ep', split_axis=0, concat_axis=0, tiled=True)  17.9 us
    unnamed x14, local copies, waits for them, and re-layouts  6.75 us
    dot_general x2, matrix products, partial_softmax(): jnp.einsum('rhk,rck->rhc', query_block, keys_all, preferred_element_type=...  5.51 us
    all_to_all x1, starting transfers between devices, body(): lax.all_to_all(ordered, 'ep', split_axis=0, concat_axis=0, tiled=True)  5.46 us
    all_to_all x1, starting transfers between devices, sent_together(): lax.all_to_all(both, axis, split_axis=split_dim, concat_axis=concat_dim,...  3.86 us
  transfers between devices with their start and end apart: 2, of which 2 were waited for; matrix products, arithmetic and copies ran while one was open for 10% of the time, Pallas kernels for 0%

commit v1 on v0

v1 whole, which is shorter than its diff:
```python
import jax
import jax.numpy as jnp
from jax import lax
from jax.sharding import PartitionSpec as P

LAT = 512
score_scale = 192.0 ** (-0.5)
neg_fill = -1e30


def sigma(g):
    return g // 2 + 16 * (g % 2)


def body(queries, latent_cache, cached_lengths, prefill_rows, owner_rank, value_up, out_proj):
    n = latent_cache.shape[0]
    context = latent_cache.shape[1]
    width = latent_cache.shape[2]
    d = lax.axis_index("ep")
    g = lax.axis_index(("hd", "rep"))
    mine = lax.rem(sigma(g) - d + n, n)
    j = jnp.sum(jnp.where(owner_rank == mine, jnp.arange(n, dtype=jnp.int32), 0))
    row = lax.dynamic_index_in_dim(prefill_rows, j, 0, keepdims=False)
    pairs = [(s * n + k, (sigma(k) - s) % n * n + k) for s in range(n) for k in range(n)]
    fresh_row = lax.ppermute(row, ("ep", "hd", "rep"), pairs)

    seats = jnp.array([sigma(k) for k in range(n)], dtype=jnp.int32)
    request_at = lax.rem(seats - d + n, n)
    choose = (request_at[:, None] == jnp.arange(n, dtype=jnp.int32)[None, :]).astype(jnp.bfloat16)
    queries_out = jnp.einsum("gr,rhk->ghk", choose, queries, preferred_element_type=jnp.float32).astype(jnp.bfloat16)
    q = lax.all_to_all(queries_out, ("hd", "rep"), split_axis=0, concat_axis=0, tiled=True)
    q = q.reshape(-1, width)
    cache_row = lax.dynamic_index_in_dim(latent_cache, mine, 0, keepdims=False)
    length = lax.dynamic_index_in_dim(cached_lengths, mine, 0, keepdims=False)
    keys = jnp.concatenate([cache_row, fresh_row], axis=0)
    scores = jnp.einsum("hk,ck->hc", q, keys, preferred_element_type=jnp.float32) * score_scale
    position = jnp.arange(keys.shape[0], dtype=jnp.int32)
    visible = (position < length) | (position >= context)
    scores = jnp.where(visible[None, :], scores, neg_fill)
    maxima = jnp.max(scores, axis=-1, keepdims=True)
    weights = jnp.exp(scores - maxima)
    totals = jnp.sum(weights, axis=-1, keepdims=True)
    summed = jnp.einsum("hc,cl->hl", weights, keys[:, :LAT], preferred_element_type=jnp.float32)
    latent = (summed / totals).astype(jnp.bfloat16)
    latent = jnp.pad(latent, ((0, 0), (0, width - LAT)))
    both = jnp.concatenate([latent.reshape(n, 2, width), fresh_row.reshape(n, 2, width)], axis=1)
    both = lax.all_to_all(both, ("hd", "rep"), split_axis=0, concat_axis=0, tiled=True)
    both = jnp.einsum("gr,ghk->rhk", choose, both, preferred_element_type=jnp.float32).astype(jnp.bfloat16)
    latent_out = both[:, :2, :LAT]
    fresh = both[:, 2:, :]
    head_out = jnp.einsum("rhl,hlv->rhv", latent_out, value_up, preferred_element_type=jnp.float32)
    head_out = head_out.astype(jnp.bfloat16).reshape(n, -1)
    partial_term = jnp.dot(head_out, out_proj, preferred_element_type=jnp.float32).astype(jnp.bfloat16)
    parts = jnp.moveaxis(partial_term.reshape(n, n, -1), 1, 0)
    arrived = lax.all_to_all(parts, ("hd", "rep"), split_axis=0, concat_axis=0, tiled=True)
    mixed = arrived.astype(jnp.float32).sum(axis=0).astype(jnp.bfloat16)
    return (mixed, fresh)


def solution(mesh):
    in_specs = (
        P("ep", ("hd", "rep"), None),
        P("ep", None, None),
        P("ep"),
        P("ep", None, None),
        P("ep"),
        P(("hd", "rep"), None, None),
        P(("hd", "rep"), None),
    )
    out_specs = (P("ep", ("hd", "rep")), P("ep", ("hd", "rep"), None))
    return jax.shard_map(body, mesh=mesh, in_specs=in_specs, out_specs=out_specs, check_vma=False)
```

time: 156 us -> 92.2 us (0.59)
  blocking collectives: 83.1 us -> 19.6 us
  starting transfers between devices: 9.32 us -> 41.2 us
  waiting for transfers between devices: 38.1 us -> 12 us
  matrix products: 13.1 us -> 6.46 us
  local copies, waits for them, and re-layouts: 9.27 us -> 6.58 us
  between operations: 0.78 us -> 2.73 us
  other arithmetic: 1.3 us -> 3.19 us
    all_to_all x2 -> x1, blocking collectives: 83.1 us -> 19.6 us  [body(): lax.all_to_all(both, ('hd', 'rep'), split_axis=0, concat_axis=0, tiled=True)]
    all_to_all x2, waiting for transfers between devices: 38.1 us -> 11 us  [the longest x1 11 us: body(): lax.all_to_all(parts, ('hd', 'rep'), split_axis=0, concat_axis=0, tiled=T...]
    ppermute x0 -> x1, starting transfers between devices: none -> 19.6 us  [body(): fresh_row = lax.ppermute(row, ('ep', 'hd', 'rep'), pairs)]
    all_to_all x2, starting transfers between devices: 9.32 us -> 21.5 us  [the longest x1 17.6 us: body(): lax.all_to_all(queries_out, ('hd', 'rep'), split_axis=0, concat_axis=0, t...]
    dot_general x10 -> x5, matrix products: 9.85 us -> 2.9 us  [the longest x1 1.11 us: body(): jnp.einsum('rhl,hlv->rhv', latent_out, value_up, preferred_element_type=j...]
    unnamed x14 -> x3, local copies, waits for them, and re-layouts: 6.75 us -> 0.71 us
    reshape x5, local copies, waits for them, and re-layouts: 1.11 us -> 3 us  [the longest x2 2.84 us: body(): parts = jnp.moveaxis(partial_term.reshape(n, n, -1), 1, 0)]
  transfers between devices with their start and end apart: 2 -> 3, of which waited for: 2 -> 2; matrix products, arithmetic and copies ran while one was open for 10% -> 4% of each run, Pallas kernels for 0% -> 0%
where the time goes in v1:
time: 92.2 us; the launch traced here: 91.7 us
  starting transfers between devices  41.2 us (45%)
  blocking collectives  19.6 us (21%)
  waiting for transfers between devices  12 us (13%)
  local copies, waits for them, and re-layouts  6.58 us (7%)
  matrix products  6.46 us (7%)
  other arithmetic  3.19 us (3%)
  between operations  2.73 us (3%)
    ppermute x1, starting transfers between devices, body(): fresh_row = lax.ppermute(row, ('ep', 'hd', 'rep'), pairs)  19.6 us
    all_to_all x1, blocking collectives, body(): lax.all_to_all(both, ('hd', 'rep'), split_axis=0, concat_axis=0, tiled=True)  19.6 us
    all_to_all x1, starting transfers between devices, body(): lax.all_to_all(queries_out, ('hd', 'rep'), split_axis=0, concat_axis=0, t...  17.6 us
    all_to_all x1, waiting for transfers between devices, body(): lax.all_to_all(parts, ('hd', 'rep'), split_axis=0, concat_axis=0, tiled=T...  11 us
    all_to_all x1, starting transfers between devices, body(): lax.all_to_all(parts, ('hd', 'rep'), split_axis=0, concat_axis=0, tiled=T...  3.9 us
    dot_general x1, matrix products, body(): jnp.dot(head_out, out_proj, preferred_element_type=jnp.float32)  3.56 us
    reshape x2, local copies, waits for them, and re-layouts, body(): parts = jnp.moveaxis(partial_term.reshape(n, n, -1), 1, 0)  2.84 us
  transfers between devices with their start and end apart: 3, of which 2 were waited for; matrix products, arithmetic and copies ran while one was open for 4% of the time, Pallas kernels for 0%

profile of v1, /device:TPU:1, one launch (start us, length us, event | category | flops | bytes accessed | tf_op | source)
XLA Modules:
  0.0 91.7 jit_solution(14111832100944091526)
XLA Ops:
  0.6 0.0 copy-start
  0.7 1.5 %compare_select_fusion = (s32[32]{0:T(128)S(1)}, s32[]{:T(128)}) fusion(s32[32]{0:T(128)} %constant.75.clone, s32[]{:T(128)S(6)} %axis_index.33, s32[32]{0:T(128)} %param.12, s32[]{:T(128)S(6)} %rem.62), kind=kLoop, calls=%fused_computation.31 | loop fusion | flops 351 | bytes 396 | tf_op jit(solution)/shard_map/rem | solution.py:28
  2.1 1.1 %convolution_convert_fusion.2 = bf16[32,2,576]{2,0,1:T(8,128)(2,1)S(1)} fusion(bf16[32,2,576]{2,1,0:T(2,128)(2,1)} %param.8, s32[32]{0:T(128)S(1)} %get-tuple-element.10), kind=kOutput, calls=%fused_computation.3 | convolution fusion | flops 2397184 | bytes 147584 | tf_op jit(solution)/shard_map/gr,rhk->ghk/dot_general | solution.py:30
  3.2 0.7 copy.23
  3.9 17.6 %all-to-all-start = ((bf16[32,2,576]{2,1,0:T(2,128)(2,1)}), bf16[32,2,576]{2,1,0:T(2,128)(2,1)S(1)}, u32[]{:S(2)}, u32[]{:S(2)}) async-start(bf16[32,2,576]{2,1,0:T(2,128)(2,1)} %copy.23), calls=%async_computation | async-start | bytes 163840 | tf_op jit(solution)/shard_map/all_to_all | solution.py:31
  23.5 0.0 copy-done
  23.5 19.6 %collective-permute-start = (bf16[64,576]{1,0:T(8,128)(2,1)S(1)}, bf16[64,576]{1,0:T(8,128)(2,1)S(1)}, u32[]{:S(2)}, u32[]{:S(2)}) collective-permute-start(bf16[64,576]{1,0:T(8,128)(2,1)S(1)} %dynamic-slice_bitcast_fusion), channel_id=1, source_target_pairs={{0,0},{1,513},{2,34},{3,547},{4,68},{5,581},{6,102},{7,615},{8,136... | collective-permute-start | bytes 221192 | tf_op jit(solution)/shard_map/ppermute | solution.py:25
  43.2 1.2 %dynamic_slice.11 = s32[1]{0:T(128)} dynamic-slice(s32[32]{0:T(128)} %param.10, s32[]{:T(128)S(6)} %select_n.30), dynamic_slice_sizes={1} | dynamic-slice | bytes 12 | tf_op jit(solution)/shard_map/jit(dynamic_index_in_dim)/dynamic_slice | solution.py:34
  44.5 0.9 dynamic-slice_bitcast_fusion.1
  45.3 0.6 compare_or_fusion
  46.0 0.0 all-to-all-done
  46.0 0.1 reshape.29
  46.1 1.0 %collective-permute-done = bf16[64,576]{1,0:T(8,128)(2,1)S(1)} collective-permute-done((bf16[64,576]{1,0:T(8,128)(2,1)S(1)}, bf16[64,576]{1,0:T(8,128)(2,1)S(1)}, u32[]{:S(2)}, u32[]{:S(2)}) %collective-permute-start) | collective-permute-done | bytes 73760 | tf_op jit(solution)/shard_map/ppermute | solution.py:25
  47.1 0.3 fusion.25
  47.4 0.2 fusion.12
  47.6 0.2 fusion
  47.9 0.2 pad_maximum_fusion
  48.1 19.6 %all_to_all.15 = bf16[32,4,576]{2,1,0:T(4,128)(2,1)S(1)} all-to-all(bf16[32,4,576]{2,1,0:T(4,128)(2,1)S(1)} %pad_maximum_fusion), channel_id=1, replica_groups=mesh['ep'=32,'hd'=4,'rep'=8] {'hd','rep'}, dimensions={0} | all-to-all | bytes 294912 | tf_op jit(solution)/shard_map/all_to_all | solution.py:47
  67.7 0.2 convolution_convert_fusion.1
  67.8 1.1 %fusion.2 = bf16[2,4,8,128]{3,2,1,0:T(8,128)(2,1)S(1)} fusion(bf16[2,512,128]{2,1,0:T(8,128)(2,1)} %param.13, bf16[32,4,576]{2,0,1:T(8,128)(2,1)S(1)} %convolution_convert_fusion.1), kind=kOutput, calls=%fused_computation.8 | convolution fusion | flops 8396800 | bytes 344064 | tf_op jit(solution)/shard_map/rhl,hlv->rhv/dot_general | solution.py:51
  69.0 3.6 %convolution_convert_fusion = bf16[32,7168]{1,0:T(8,128)(2,1)} fusion(bf16[256,7168]{1,0:T(8,128)(2,1)} %param.14, bf16[2,4,8,128]{3,2,1,0:T(8,128)(2,1)S(1)} %fusion.2), kind=kOutput, calls=%fused_computation | convolution fusion | flops 117669888 | bytes 4145152 | tf_op jit(solution)/shard_map/dot_general | solution.py:53
  72.5 1.8 %reshape.33 = bf16[32,32,224]{2,1,0:T(8,128)(2,1)S(1)} reshape(bf16[32,7168]{1,0:T(8,128)(2,1)} %convolution_convert_fusion) | data formatting | bytes 917504 | tf_op jit(solution)/shard_map/reshape | solution.py:54
  74.3 1.1 %copy.40 = bf16[32,32,224]{2,0,1:T(8,128)(2,1)} copy(bf16[32,32,224]{2,1,0:T(8,128)(2,1)S(1)} %reshape.33) | data formatting | bytes 917504 | tf_op jit(solution)/shard_map/reshape | solution.py:54
  75.4 3.9 %all-to-all-start.2 = ((bf16[32,32,224]{2,1,0:T(8,128)(2,1)}), bf16[32,32,224]{2,1,0:T(8,128)(2,1)S(1)}, u32[]{:S(2)}, u32[]{:S(2)}) async-start(bf16[32,32,224]{2,1,0:T(8,128)(2,1)} %bitcast.22), calls=%async_computation.2 | async-start | bytes 1048576 | tf_op jit(solution)/shard_map/all_to_all | solution.py:55
  79.3 0.7 copy.27
  80.0 11.0 %all-to-all-done.2 = bf16[32,32,224]{2,1,0:T(8,128)(2,1)S(1)} async-done(((bf16[32,32,224]{2,1,0:T(8,128)(2,1)}), bf16[32,32,224]{2,1,0:T(8,128)(2,1)S(1)}, u32[]{:S(2)}, u32[]{:S(2)}) %all-to-all-start.2) | async-done | bytes 458784 | tf_op jit(solution)/shard_map/all_to_all | solution.py:55
  91.0 0.7 reduce_sum.32
  (5 shorter events, 0.1 us)
Async XLA Ops:
  0.6 22.9 %copy-start = (bf16[32,64,576]{2,1,0:T(8,128)(2,1)S(1)}, bf16[32,64,576]{2,1,0:T(8,128)(2,1)}, u32[]{:S(2)}) copy-start(bf16[32,64,576]{2,1,0:T(8,128)(2,1)} %param.11) | copy-start | bytes 7077892
  3.9 42.1 %all-to-all-start = ((bf16[32,2,576]{2,1,0:T(2,128)(2,1)}), bf16[32,2,576]{2,1,0:T(2,128)(2,1)S(1)}, u32[]{:S(2)}, u32[]{:S(2)}) async-start(bf16[32,2,576]{2,1,0:T(2,128)(2,1)} %copy.23), calls=%async_computation | async-start | bytes 163840 | tf_op jit(solution)/shard_map/all_to_all | solution.py:31
  23.5 23.5 %collective-permute-start = (bf16[64,576]{1,0:T(8,128)(2,1)S(1)}, bf16[64,576]{1,0:T(8,128)(2,1)S(1)}, u32[]{:S(2)}, u32[]{:S(2)}) collective-permute-start(bf16[64,576]{1,0:T(8,128)(2,1)S(1)} %dynamic-slice_bitcast_fusion), channel_id=1, source_target_pairs={{0,0},{1,513},{2,34},{3,547},{4,68},{5,581},{6,102},{7,615},{8,136... | collective-permute-start | bytes 221192 | tf_op jit(solution)/shard_map/ppermute | solution.py:25
  75.4 15.6 %all-to-all-start.2 = ((bf16[32,32,224]{2,1,0:T(8,128)(2,1)}), bf16[32,32,224]{2,1,0:T(8,128)(2,1)S(1)}, u32[]{:S(2)}, u32[]{:S(2)}) async-start(bf16[32,32,224]{2,1,0:T(8,128)(2,1)} %bitcast.22), calls=%async_computation.2 | async-start | bytes 1048576 | tf_op jit(solution)/shard_map/all_to_all | solution.py:55

commit v2 on v1

--- a/solution.py
+++ b/solution.py
@@ -1,7 +1,10 @@
 import jax
 import jax.numpy as jnp
 from jax import lax
+from jax.experimental import pallas as pl
+from jax.experimental.pallas import tpu as pltpu
 from jax.sharding import PartitionSpec as P
+
 
 LAT = 512
 score_scale = 192.0 ** (-0.5)
@@ -12,24 +15,64 @@
     return g // 2 + 16 * (g % 2)
 
 
+def seat_request(n):
+    d = lax.axis_index("ep")
+    g = lax.axis_index("hd") * lax.axis_size("rep") + lax.axis_index("rep")
+    return lax.rem(lax.div(g, 2) + (n // 2) * lax.rem(g, 2) - d + n, n)
+
+
+def pick_kernel(owner_ref, rows_ref, after_ref, row_ref, sem):
+    n = rows_ref.shape[0]
+    mine = seat_request(n)
+    j = jnp.int32(0)
+    for i in range(n):
+        j = jnp.where(owner_ref[i] == mine, jnp.int32(i), j)
+    copy = pltpu.make_async_copy(rows_ref.at[j], row_ref, sem)
+    copy.start()
+    copy.wait()
+
+
+def pick_row(owner_rank, prefill_rows, after):
+    return pl.pallas_call(
+        pick_kernel,
+        out_shape=jax.ShapeDtypeStruct(prefill_rows.shape[1:], prefill_rows.dtype),
+        in_specs=[
+            pl.BlockSpec(memory_space=pltpu.SMEM),
+            pl.BlockSpec(memory_space=pl.ANY),
+            pl.BlockSpec(memory_space=pl.ANY),
+        ],
+        out_specs=pl.BlockSpec(memory_space=pltpu.VMEM),
+        scratch_shapes=[pltpu.SemaphoreType.DMA],
+        name="pick_row",
+    )(owner_rank, prefill_rows, after)
+
+
 def body(queries, latent_cache, cached_lengths, prefill_rows, owner_rank, value_up, out_proj):
     n = latent_cache.shape[0]
     context = latent_cache.shape[1]
     width = latent_cache.shape[2]
     d = lax.axis_index("ep")
-    g = lax.axis_index(("hd", "rep"))
-    mine = lax.rem(sigma(g) - d + n, n)
-    j = jnp.sum(jnp.where(owner_rank == mine, jnp.arange(n, dtype=jnp.int32), 0))
-    row = lax.dynamic_index_in_dim(prefill_rows, j, 0, keepdims=False)
+    mine = seat_request(n)
     pairs = [(s * n + k, (sigma(k) - s) % n * n + k) for s in range(n) for k in range(n)]
+    seats = jnp.array([sigma(k) for k in range(n)], dtype=jnp.int32)
+
+    def choice():
+        request_at = lax.rem(seats - d + n, n)
+        return (request_at[:, None] == jnp.arange(n, dtype=jnp.int32)[None, :]).astype(jnp.bfloat16)
+
+    def spread(value):
+        ordered = jnp.einsum("gr,rhk->ghk", choice(), value, preferred_element_type=jnp.float32)
+        return lax.all_to_all(
+            ordered.astype(jnp.bfloat16), ("hd", "rep"), split_axis=0, concat_axis=0, tiled=True
+        )
+
+    early = (d <= 9) | (d >= 26)
+    q_first = lax.cond(early, spread, lambda value: jnp.zeros_like(value), queries)
+    row = pick_row(owner_rank, prefill_rows, q_first)
     fresh_row = lax.ppermute(row, ("ep", "hd", "rep"), pairs)
-
-    seats = jnp.array([sigma(k) for k in range(n)], dtype=jnp.int32)
-    request_at = lax.rem(seats - d + n, n)
-    choose = (request_at[:, None] == jnp.arange(n, dtype=jnp.int32)[None, :]).astype(jnp.bfloat16)
-    queries_out = jnp.einsum("gr,rhk->ghk", choose, queries, preferred_element_type=jnp.float32).astype(jnp.bfloat16)
-    q = lax.all_to_all(queries_out, ("hd", "rep"), split_axis=0, concat_axis=0, tiled=True)
+    q = lax.cond(early, lambda had, value: had, lambda had, value: spread(value), q_first, queries)
     q = q.reshape(-1, width)
+    choose = choice()
     cache_row = lax.dynamic_index_in_dim(latent_cache, mine, 0, keepdims=False)
     length = lax.dynamic_index_in_dim(cached_lengths, mine, 0, keepdims=False)
     keys = jnp.concatenate([cache_row, fresh_row], axis=0)
@@ -68,4 +111,5 @@
         P(("hd", "rep"), None),
     )
     out_specs = (P("ep", ("hd", "rep")), P("ep", ("hd", "rep"), None))
+
     return jax.shard_map(body, mesh=mesh, in_specs=in_specs, out_specs=out_specs, check_vma=False)

time: 92.2 us -> 88.8 us (0.963)
  starting transfers between devices: 41.2 us -> 11 us
  waiting for transfers between devices: 12 us -> 36.1 us
  blocking collectives: 19.6 us -> 24.3 us
  Pallas kernels: 0 us -> 2.23 us
  local copies, waits for them, and re-layouts: 6.58 us -> 4.42 us
  between operations: 2.73 us -> 0.8 us
  matrix products: 6.46 us -> 5.53 us
    ppermute x1, waiting for transfers between devices: 0.97 us -> 19.2 us  [body(): fresh_row = lax.ppermute(row, ('ep', 'hd', 'rep'), pairs)]
    ppermute x1, starting transfers between devices: 19.6 us -> 3.43 us  [body(): fresh_row = lax.ppermute(row, ('ep', 'hd', 'rep'), pairs)]
    all_to_all x1, starting transfers between devices: 17.6 us -> 3.65 us  [body(): lax.all_to_all(both, ('hd', 'rep'), split_axis=0, concat_axis=0, tiled=True)]
    all_to_all x1, waiting for transfers between devices: 0.01 us -> 5.95 us  [body(): lax.all_to_all(both, ('hd', 'rep'), split_axis=0, concat_axis=0, tiled=True)]
    all_to_all x1, blocking collectives: 19.6 us -> 24.3 us  [spread(): lax.all_to_all(ordered.astype(jnp.bfloat16), ('hd', 'rep'), split_axis=0,...]
    pallas_call x0 -> x1, Pallas kernels: none -> 2.23 us  [pick_row(): pl.pallas_call(pick_kernel, out_shape=jax.ShapeDtypeStruct(prefill_rows.s...]
    dot_general x1, matrix products: 1.11 us -> 0.15 us  [body(): jnp.einsum('rhl,hlv->rhv', latent_out, value_up, preferred_element_type=j...]
  transfers between devices with their start and end apart: 3 -> 3, of which waited for: 2 -> 3; matrix products, arithmetic and copies ran while one was open for 4% -> 3% of each run, Pallas kernels for 0% -> 0%
where the time goes in v2:
time: 88.8 us; the launch traced here: 88.2 us
  waiting for transfers between devices  36.1 us (41%)
  blocking collectives  24.3 us (27%)
  starting transfers between devices  11 us (12%)
  matrix products  5.53 us (6%)
  local copies, waits for them, and re-layouts  4.42 us (5%)
  other arithmetic  3.83 us (4%)
  Pallas kernels  2.23 us (3%)
    all_to_all x1, blocking collectives, spread(): lax.all_to_all(ordered.astype(jnp.bfloat16), ('hd', 'rep'), split_axis=0,...  24.3 us
    ppermute x1, waiting for transfers between devices, body(): fresh_row = lax.ppermute(row, ('ep', 'hd', 'rep'), pairs)  19.2 us
    all_to_all x1, waiting for transfers between devices, body(): lax.all_to_all(parts, ('hd', 'rep'), split_axis=0, concat_axis=0, tiled=T...  11 us
    all_to_all x1, waiting for transfers between devices, body(): lax.all_to_all(both, ('hd', 'rep'), split_axis=0, concat_axis=0, tiled=True)  5.95 us
    all_to_all x1, starting transfers between devices, body(): lax.all_to_all(parts, ('hd', 'rep'), split_axis=0, concat_axis=0, tiled=T...  3.9 us
    all_to_all x1, starting transfers between devices, body(): lax.all_to_all(both, ('hd', 'rep'), split_axis=0, concat_axis=0, tiled=True)  3.65 us
    dot_general x1, matrix products, body(): jnp.dot(head_out, out_proj, preferred_element_type=jnp.float32)  3.57 us
    ppermute x1, starting transfers between devices, body(): fresh_row = lax.ppermute(row, ('ep', 'hd', 'rep'), pairs)  3.43 us
  transfers between devices with their start and end apart: 3, of which 3 were waited for; matrix products, arithmetic and copies ran while one was open for 3% of the time, Pallas kernels for 0%

profile of v2, /device:TPU:1, one launch (start us, length us, event | category | flops | bytes accessed | tf_op | source)
XLA Modules:
  0.0 88.2 jit_solution(16187053684609197900)
XLA Ops:
  0.6 0.0 copy-start
  0.6 0.0 copy-start.2
  0.7 0.0 copy-start.1
  0.7 26.3 %conditional.2 = (bf16[32,2,576]{2,1,0:T(2,128)(2,1)S(1)}) conditional(s32[]{:T(128)} %convert_element_type.32, () %tuple.23, (s32[]{:T(128)}, s32[32]{0:T(128)}, bf16[32,2,576]{2,1,0:T(2,128)(2,1)}) %tuple.26), branch_computations={%region_0.0_spmd, %region_1.0_spmd} | conditional | flops 2397440 | bytes 442764 | solution.py:70
  0.7 0.8 compare_select_fusion
  1.5 1.1 %convolution_convert_fusion = bf16[32,2,576]{2,0,1:T(8,128)(2,1)S(1)} fusion(bf16[32,2,576]{2,1,0:T(2,128)(2,1)} %get-tuple-element.47, s32[32]{0:T(128)S(1)} %compare_select_fusion), kind=kOutput, calls=%fused_computation | convolution fusion | flops 2397184 | bytes 147584 | tf_op jit(solution)/shard_map/cond/branch_1_fun/gr,rhk->ghk/dot_general | solution.py:64
  2.6 0.1 copy.26
  2.7 24.3 %all_to_all.18 = bf16[32,2,576]{2,1,0:T(2,128)(2,1)S(1)} all-to-all(bf16[32,2,576]{2,1,0:T(2,128)(2,1)S(1)} %copy.26), channel_id=1, replica_groups=mesh['ep'=32,'hd'=4,'rep'=8] {'hd','rep'}, dimensions={0} | all-to-all | bytes 147456 | tf_op jit(solution)/shard_map/cond/branch_1_fun/all_to_all | solution.py:65
  27.0 2.2 %pick_row.1 = bf16[64,576]{1,0:T(8,128)(2,1)} custom-call(s32[32]{0:T(128)} %owner_ref.1, bf16[32,64,576]{2,1,0:T(8,128)(2,1)} %rows_ref.1, bf16[32,2,576]{2,1,0:T(2,128)(2,1)S(1)} %get-tuple-element.55.after_ref), custom_call_target="tpu_custom_call" | custom-call | tf_op jit(solution)/shard_map/pick_row/pallas_call | solution.py:36
  29.2 3.4 %collective-permute-start = (bf16[64,576]{1,0:T(8,128)(2,1)}, bf16[64,576]{1,0:T(8,128)(2,1)S(1)}, u32[]{:S(2)}, u32[]{:S(2)}) collective-permute-start(bf16[64,576]{1,0:T(8,128)(2,1)} %pick_row.1), channel_id=1, source_target_pairs={{0,0},{1,513},{2,34},{3,547},{4,68},{5,581},{6,102},{7,615},{8,136... | collective-permute-start | bytes 221192 | tf_op jit(solution)/shard_map/ppermute | solution.py:72
  32.7 0.1 conditional.3
  32.7 0.1 reshape.30
  32.8 0.6 dynamic_slice.8
  33.4 0.6 compare_or_fusion
  34.0 19.2 %collective-permute-done = bf16[64,576]{1,0:T(8,128)(2,1)S(1)} collective-permute-done((bf16[64,576]{1,0:T(8,128)(2,1)}, bf16[64,576]{1,0:T(8,128)(2,1)S(1)}, u32[]{:S(2)}, u32[]{:S(2)}) %collective-permute-start) | collective-permute-done | bytes 73760 | tf_op jit(solution)/shard_map/ppermute | solution.py:72
  53.2 0.3 fusion.31
  53.5 0.2 fusion.21
  53.7 0.2 fusion.10
  54.0 0.8 pad_maximum_fusion
  54.9 3.6 %all-to-all-start.2 = ((bf16[32,4,576]{2,1,0:T(4,128)(2,1)}), bf16[32,4,576]{2,1,0:T(4,128)(2,1)S(1)}, u32[]{:S(2)}, u32[]{:S(2)}) async-start(bf16[32,4,576]{2,1,0:T(4,128)(2,1)} %pad_maximum_fusion), calls=%async_computation.2 | async-start | bytes 327680 | tf_op jit(solution)/shard_map/all_to_all | solution.py:90
  58.5 0.7 compare_select_fusion.4
  59.2 6.0 %all-to-all-done.2 = bf16[32,4,576]{2,1,0:T(4,128)(2,1)S(1)} async-done(((bf16[32,4,576]{2,1,0:T(4,128)(2,1)}), bf16[32,4,576]{2,1,0:T(4,128)(2,1)S(1)}, u32[]{:S(2)}, u32[]{:S(2)}) %all-to-all-start.2) | async-done | bytes 147488 | tf_op jit(solution)/shard_map/all_to_all | solution.py:90
  65.2 0.2 convolution_convert_fusion.3
  65.3 0.0 copy-done.1
  65.4 0.2 fusion.12
  65.5 3.6 %convolution_convert_fusion.2 = bf16[32,7168]{1,0:T(8,128)(2,1)} fusion(bf16[256,7168]{1,0:T(8,128)(2,1)} %param.18, bf16[2,4,8,128]{3,2,1,0:T(8,128)(2,1)S(1)} %fusion.12), kind=kOutput, calls=%fused_computation.16 | convolution fusion | flops 117669888 | bytes 4145152 | tf_op jit(solution)/shard_map/dot_general | solution.py:96
  69.1 1.8 %reshape.38 = bf16[32,32,224]{2,1,0:T(8,128)(2,1)S(1)} reshape(bf16[32,7168]{1,0:T(8,128)(2,1)} %convolution_convert_fusion.2) | data formatting | bytes 917504 | tf_op jit(solution)/shard_map/reshape | solution.py:97
  70.8 1.1 %copy.46 = bf16[32,32,224]{2,0,1:T(8,128)(2,1)} copy(bf16[32,32,224]{2,1,0:T(8,128)(2,1)S(1)} %reshape.38) | data formatting | bytes 917504 | tf_op jit(solution)/shard_map/reshape | solution.py:97
  71.9 3.9 %all-to-all-start.3 = ((bf16[32,32,224]{2,1,0:T(8,128)(2,1)}), bf16[32,32,224]{2,1,0:T(8,128)(2,1)S(1)}, u32[]{:S(2)}, u32[]{:S(2)}) async-start(bf16[32,32,224]{2,1,0:T(8,128)(2,1)} %bitcast.24), calls=%async_computation.3 | async-start | bytes 1048576 | tf_op jit(solution)/shard_map/all_to_all | solution.py:98
  75.8 0.7 copy.33
  76.5 11.0 %all-to-all-done.3 = bf16[32,32,224]{2,1,0:T(8,128)(2,1)S(1)} async-done(((bf16[32,32,224]{2,1,0:T(8,128)(2,1)}), bf16[32,32,224]{2,1,0:T(8,128)(2,1)S(1)}, u32[]{:S(2)}, u32[]{:S(2)}) %all-to-all-start.3) | async-done | bytes 458784 | tf_op jit(solution)/shard_map/all_to_all | solution.py:98
  87.5 0.7 reduce_sum.22
  (7 shorter events, 0.1 us)
Async XLA Ops:
  0.6 32.8 %copy-start = (bf16[32,64,576]{2,1,0:T(8,128)(2,1)S(1)}, bf16[32,64,576]{2,1,0:T(8,128)(2,1)}, u32[]{:S(2)}) copy-start(bf16[32,64,576]{2,1,0:T(8,128)(2,1)} %param.13) | copy-start | bytes 7077892
  0.6 32.1 %copy-start.2 = (s32[32]{0:T(128)S(1)}, s32[32]{0:T(128)}, u32[]{:S(2)}) copy-start(s32[32]{0:T(128)} %param.14) | copy-start | bytes 388
  0.7 64.7 %copy-start.1 = (bf16[2,512,128]{2,1,0:T(8,128)(2,1)S(1)}, bf16[2,512,128]{2,1,0:T(8,128)(2,1)}, u32[]{:S(2)}) copy-start(bf16[2,512,128]{2,1,0:T(8,128)(2,1)} %param.17) | copy-start | bytes 786436
  29.2 24.0 %collective-permute-start = (bf16[64,576]{1,0:T(8,128)(2,1)}, bf16[64,576]{1,0:T(8,128)(2,1)S(1)}, u32[]{:S(2)}, u32[]{:S(2)}) collective-permute-start(bf16[64,576]{1,0:T(8,128)(2,1)} %pick_row.1), channel_id=1, source_target_pairs={{0,0},{1,513},{2,34},{3,547},{4,68},{5,581},{6,102},{7,615},{8,136... | collective-permute-start | bytes 221192 | tf_op jit(solution)/shard_map/ppermute | solution.py:72
  54.9 10.3 %all-to-all-start.2 = ((bf16[32,4,576]{2,1,0:T(4,128)(2,1)}), bf16[32,4,576]{2,1,0:T(4,128)(2,1)S(1)}, u32[]{:S(2)}, u32[]{:S(2)}) async-start(bf16[32,4,576]{2,1,0:T(4,128)(2,1)} %pad_maximum_fusion), calls=%async_computation.2 | async-start | bytes 327680 | tf_op jit(solution)/shard_map/all_to_all | solution.py:90
  71.9 15.6 %all-to-all-start.3 = ((bf16[32,32,224]{2,1,0:T(8,128)(2,1)}), bf16[32,32,224]{2,1,0:T(8,128)(2,1)S(1)}, u32[]{:S(2)}, u32[]{:S(2)}) async-start(bf16[32,32,224]{2,1,0:T(8,128)(2,1)} %bitcast.24), calls=%async_computation.3 | async-start | bytes 1048576 | tf_op jit(solution)/shard_map/all_to_all | solution.py:98

commit v3 on v2

v3 whole, which is shorter than its diff:
```python
import jax
import jax.numpy as jnp
from jax import lax
from jax.experimental import pallas as pl
from jax.experimental.pallas import tpu as pltpu
from jax.sharding import PartitionSpec as P


LAT = 512
score_scale = 192.0 ** (-0.5)
neg_fill = -1e30
VMEM = pl.BlockSpec(memory_space=pltpu.VMEM)
SMEM = pl.BlockSpec(memory_space=pltpu.SMEM)
ANY = pl.BlockSpec(memory_space=pl.ANY)


def sigma(g):
    return g // 2 + 16 * (g % 2)


def seat_request(n):
    d = lax.axis_index("ep")
    g = lax.axis_index("hd") * lax.axis_size("rep") + lax.axis_index("rep")
    return lax.rem(lax.div(g, 2) + (n // 2) * lax.rem(g, 2) - d + n, n)


def leaving(z, n):
    half = n // 2
    rank = 12 * z * (z <= half) + (12 * half - 5 * (z - half)) * (z > half)
    return rank * n + z


def pick_kernel(owner_ref, rows_ref, row_ref, sem):
    n = rows_ref.shape[0]
    mine = seat_request(n)
    j = jnp.int32(0)
    for i in range(n):
        j = jnp.where(owner_ref[i] == mine, jnp.int32(i), j)
    copy = pltpu.make_async_copy(rows_ref.at[j], row_ref, sem)
    copy.start()
    copy.wait()


def pick_row(owner_rank, prefill_rows):
    return pl.pallas_call(
        pick_kernel,
        out_shape=jax.ShapeDtypeStruct(prefill_rows.shape[1:], prefill_rows.dtype),
        in_specs=[SMEM, ANY],
        out_specs=VMEM,
        scratch_shapes=[pltpu.SemaphoreType.DMA],
        name="pick_row",
    )(owner_rank, prefill_rows)


def cached_kernel(lengths_ref, cache_ref, row_ref, bias_ref, sem):
    mine = seat_request(cache_ref.shape[0])
    copy = pltpu.make_async_copy(cache_ref.at[mine], row_ref, sem)
    copy.start()
    position = lax.broadcasted_iota(jnp.int32, bias_ref.shape, 1)
    visible = (position < lengths_ref[mine]) | (position >= cache_ref.shape[1])
    bias_ref[...] = jnp.where(visible, 0.0, neg_fill)
    copy.wait()


def pick_cached(cached_lengths, latent_cache, positions):
    return pl.pallas_call(
        cached_kernel,
        out_shape=(
            jax.ShapeDtypeStruct(latent_cache.shape[1:], latent_cache.dtype),
            jax.ShapeDtypeStruct((8, positions), jnp.float32),
        ),
        in_specs=[SMEM, ANY],
        out_specs=(VMEM, VMEM),
        scratch_shapes=[pltpu.SemaphoreType.DMA],
        name="pick_cached",
    )(cached_lengths, latent_cache)


def project_kernel(latent_ref, up_ref, out_proj_ref, parts_ref, weights, sems):
    _, _, columns = parts_ref.shape
    steps, _, wide = weights.shape
    each = wide // columns
    copies = []
    for i in range(steps):
        window = out_proj_ref.at[:, pl.ds(i * wide, wide)]
        copies.append(pltpu.make_async_copy(window, weights.at[i], sems.at[i]))
        copies[i].start()
    heads = [
        jnp.dot(latent_ref[i, :, :LAT], up_ref[i], preferred_element_type=jnp.float32)
        for i in range(up_ref.shape[0])
    ]
    head_out = jnp.concatenate(heads, axis=1).astype(jnp.bfloat16)
    for i in range(steps):
        copies[i].wait()
        term = jnp.dot(head_out, weights[i], preferred_element_type=jnp.float32)
        for k in range(each):
            piece = term[:, k * columns : (k + 1) * columns]
            parts_ref[each * i + k] = piece.astype(jnp.bfloat16)


def project(latent, value_up, out_proj, n):
    depth, width = out_proj.shape
    steps = n // 4
    return pl.pallas_call(
        project_kernel,
        out_shape=jax.ShapeDtypeStruct((n, latent.shape[1], width // n), jnp.bfloat16),
        in_specs=[VMEM, VMEM, ANY],
        out_specs=VMEM,
        scratch_shapes=[
            pltpu.VMEM((steps, depth, width // steps), jnp.bfloat16),
            pltpu.SemaphoreType.DMA((steps,)),
        ],
        cost_estimate=pl.CostEstimate(
            flops=2 * latent.shape[1] * depth * width,
            bytes_accessed=2 * depth * width,
            transcendentals=0,
        ),
        name="project",
    )(latent, value_up, out_proj)


def body(queries, latent_cache, cached_lengths, prefill_rows, owner_rank, value_up, out_proj):
    n = latent_cache.shape[0]
    width = latent_cache.shape[2]
    positions = latent_cache.shape[1] + prefill_rows.shape[1]
    d = lax.axis_index("ep")
    mine = seat_request(n)
    later, sooner = [], []
    for source in range(n):
        for k in range(n):
            owner = (sigma(k) - source) % n
            pair = (source * n + k, owner * n + k)
            (later if leaving(source, n) >= leaving(owner, n) else sooner).append(pair)
    from_later = leaving(mine, n) >= leaving(d, n)
    seats = jnp.array([sigma(k) for k in range(n)], dtype=jnp.int32)

    def choice():
        request_at = lax.rem(seats - d + n, n)
        return (request_at[:, None] == jnp.arange(n, dtype=jnp.int32)[None, :]).astype(jnp.bfloat16)

    def prepare(queries, cached_lengths, latent_cache):
        ordered = jnp.einsum("gr,rhk->ghk", choice(), queries, preferred_element_type=jnp.float32)
        q = lax.all_to_all(
            ordered.astype(jnp.bfloat16), ("hd", "rep"), split_axis=0, concat_axis=0, tiled=True
        )
        cache_row, bias = pick_cached(cached_lengths, latent_cache, positions)
        return q.reshape(-1, width), cache_row, bias

    def nothing(queries, cached_lengths, latent_cache):
        return (
            jnp.zeros((queries.shape[1] * n, width), queries.dtype),
            jnp.zeros(latent_cache.shape[1:], latent_cache.dtype),
            jnp.zeros((8, positions), jnp.float32),
        )

    early = (d <= 9 * n // 32) | (d >= 26 * n // 32)
    row = pick_row(owner_rank, prefill_rows)
    operands = (queries, cached_lengths, latent_cache)
    late_row = lax.ppermute(row, ("ep", "hd", "rep"), later)
    had = lax.cond(early, prepare, nothing, *operands)
    early_row = lax.ppermute(row, ("ep", "hd", "rep"), sooner)
    q, cache_row, bias = lax.cond(
        early, lambda had, operands: had, lambda had, operands: prepare(*operands), had, operands
    )
    fresh_row = jnp.where(from_later, late_row, early_row)
    keys = jnp.concatenate([cache_row, fresh_row], axis=0)
    scores = jnp.einsum("hk,ck->hc", q, keys, preferred_element_type=jnp.float32) * score_scale
    scores = scores + bias[:1]
    maxima = jnp.max(scores, axis=-1, keepdims=True)
    weights = jnp.exp(scores - maxima)
    totals = jnp.sum(weights, axis=-1, keepdims=True)
    summed = jnp.einsum("hc,cl->hl", weights, keys[:, :LAT], preferred_element_type=jnp.float32)
    latent = (summed / totals).astype(jnp.bfloat16)
    latent = jnp.pad(latent, ((0, 0), (0, width - LAT)))
    both = jnp.concatenate([latent.reshape(n, 2, width), fresh_row.reshape(n, 2, width)], axis=1)
    both = lax.all_to_all(both, ("hd", "rep"), split_axis=0, concat_axis=0, tiled=True)
    both = jnp.einsum("gr,ghk->rhk", choice(), both, preferred_element_type=jnp.float32)
    both = both.astype(jnp.bfloat16)
    fresh = both[:, 2:, :]
    parts = project(jnp.moveaxis(both, 1, 0), value_up, out_proj, n)
    arrived = lax.all_to_all(parts, ("hd", "rep"), split_axis=0, concat_axis=0, tiled=True)
    mixed = arrived.astype(jnp.float32).sum(axis=0).astype(jnp.bfloat16)
    return (mixed, fresh)


def solution(mesh):
    in_specs = (
        P("ep", ("hd", "rep"), None),
        P("ep", None, None),
        P("ep"),
        P("ep", None, None),
        P("ep"),
        P(("hd", "rep"), None, None),
        P(("hd", "rep"), None),
    )
    out_specs = (P("ep", ("hd", "rep")), P("ep", ("hd", "rep"), None))

    return jax.shard_map(body, mesh=mesh, in_specs=in_specs, out_specs=out_specs, check_vma=False)
```

time: 88.8 us -> 93.6 us (1.054)
  starting transfers between devices: 11 us -> 44.6 us
  blocking collectives: 24.3 us -> 0 us
  Pallas kernels: 2.23 us -> 8.2 us
  matrix products: 5.53 us -> 1.57 us
  local copies, waits for them, and re-layouts: 4.42 us -> 1.59 us
  other arithmetic: 3.83 us -> 1.78 us
  waiting for transfers between devices: 36.1 us -> 34.5 us
    ppermute x1 -> x2, starting transfers between devices: 3.43 us -> 30.8 us  [the longest x1 29.5 us: body(): early_row = lax.ppermute(row, ('ep', 'hd', 'rep'), sooner)]
    all_to_all x1 -> x0, blocking collectives: 24.3 us -> none  [spread(): lax.all_to_all(ordered.astype(jnp.bfloat16), ('hd', 'rep'), split_axis=0,...]
    ppermute x1 -> x2, waiting for transfers between devices: 19.2 us -> 8.83 us  [the longest x1 8.82 us: body(): late_row = lax.ppermute(row, ('ep', 'hd', 'rep'), later)]
    all_to_all x0 -> x1, waiting for transfers between devices: none -> 6.72 us  [prepare(): lax.all_to_all(ordered.astype(jnp.bfloat16), ('hd', 'rep'), split_axis=0,...]
    pallas_call x0 -> x2, Pallas kernels: none -> 5.83 us  [the longest x1 5.15 us: project(): pl.pallas_call(project_kernel, out_shape=jax.ShapeDtypeStruct((n, latent....]
    all_to_all x0 -> x1, starting transfers between devices: none -> 5.03 us  [prepare(): lax.all_to_all(ordered.astype(jnp.bfloat16), ('hd', 'rep'), split_axis=0,...]
    dot_general x4 -> x2, matrix products: 5.01 us -> 1.06 us  [the longest x1 0.84 us: body(): jnp.einsum('gr,ghk->rhk', choice(), both, preferred_element_type=jnp.floa...]
    reshape x3 -> x1, local copies, waits for them, and re-layouts: 2.91 us -> 0.07 us  [prepare(): return (q.reshape(-1, width), cache_row, bias)]
  transfers between devices with their start and end apart: 3 -> 5, of which waited for: 3 -> 4; matrix products, arithmetic and copies ran while one was open for 3% -> 2% of each run, Pallas kernels for 0% -> 1%
where the time goes in v3:
time: 93.6 us; the launch traced here: 93.1 us
  starting transfers between devices  44.6 us (48%)
  waiting for transfers between devices  34.5 us (37%)
  Pallas kernels  8.2 us (9%)
  other arithmetic  1.78 us (2%)
  local copies, waits for them, and re-layouts  1.59 us (2%)
  matrix products  1.57 us (2%)
    ppermute x1, starting transfers between devices, body(): early_row = lax.ppermute(row, ('ep', 'hd', 'rep'), sooner)  29.5 us
    all_to_all x1, waiting for transfers between devices, body(): lax.all_to_all(parts, ('hd', 'rep'), split_axis=0, concat_axis=0, tiled=T...  11 us
    ppermute x1, waiting for transfers between devices, body(): late_row = lax.ppermute(row, ('ep', 'hd', 'rep'), later)  8.82 us
    all_to_all x1, waiting for transfers between devices, body(): lax.all_to_all(both, ('hd', 'rep'), split_axis=0, concat_axis=0, tiled=True)  7.96 us
    all_to_all x1, waiting for transfers between devices, prepare(): lax.all_to_all(ordered.astype(jnp.bfloat16), ('hd', 'rep'), split_axis=0,...  6.72 us
    pallas_call x1, Pallas kernels, project(): pl.pallas_call(project_kernel, out_shape=jax.ShapeDtypeStruct((n, latent....  5.15 us
    all_to_all x1, starting transfers between devices, prepare(): lax.all_to_all(ordered.astype(jnp.bfloat16), ('hd', 'rep'), split_axis=0,...  5.03 us
    all_to_all x1, starting transfers between devices, body(): lax.all_to_all(both, ('hd', 'rep'), split_axis=0, concat_axis=0, tiled=True)  4.85 us
  transfers between devices with their start and end apart: 5, of which 4 were waited for; matrix products, arithmetic and copies ran while one was open for 2% of the time, Pallas kernels for 1%

profile of v3, /device:TPU:1, one launch (start us, length us, event | category | flops | bytes accessed | tf_op | source)
XLA Modules:
  0.0 93.1 jit_solution(9662922692288439771)
XLA Ops:
  0.6 0.0 copy-start.4
  0.6 0.0 copy-start.3
  0.7 0.0 copy-start
  0.7 0.0 copy-start.2
  0.7 2.4 %pick_row.1 = bf16[64,576]{1,0:T(8,128)(2,1)} custom-call(s32[32]{0:T(128)} %owner_ref.1, bf16[32,64,576]{2,1,0:T(8,128)(2,1)} %rows_ref.1), custom_call_target="tpu_custom_call" | custom-call | tf_op jit(solution)/shard_map/pick_row/pallas_call | solution.py:45
  3.0 29.5 %collective-permute-start.1 = (bf16[64,576]{1,0:T(8,128)(2,1)}, bf16[64,576]{1,0:T(8,128)(2,1)S(1)}, u32[]{:S(2)}, u32[]{:S(2)}) collective-permute-start(bf16[64,576]{1,0:T(8,128)(2,1)} %pick_row.1), channel_id=1, source_target_pairs={{1,513},{2,34},{3,547},{4,68},{5,581},{6,102},{7,615},{8,136},{9,6... | collective-permute-start | bytes 221192 | tf_op jit(solution)/shard_map/ppermute | solution.py:161
  32.6 1.3 %collective-permute-start = (bf16[64,576]{1,0:T(8,128)(2,1)}, bf16[64,576]{1,0:T(8,128)(2,1)S(1)}, u32[]{:S(2)}, u32[]{:S(2)}) collective-permute-start(bf16[64,576]{1,0:T(8,128)(2,1)} %pick_row.1), channel_id=1, source_target_pairs={{0,0},{34,2},{36,36},{68,4},{70,38},{72,72},{102,6},{104,40},{106,... | collective-permute-start | bytes 221192 | tf_op jit(solution)/shard_map/ppermute | solution.py:159
  33.9 0.0 copy-done.4
  33.9 0.0 copy-done.3
  33.9 0.0 copy-done
  33.9 0.0 copy-done.2
  33.9 13.5 %conditional.2 = (bf16[64,576]{1,0:T(8,128)(2,1)S(1)}, bf16[64,576]{1,0:T(8,128)(2,1)S(1)}, f32[8,128]{1,0:T(8,128)S(1)}) conditional(s32[]{:T(128)} %convert_element_type.20, () %tuple.23, (s32[]{:T(128)}, s32[32]{0:T(128)S(1)}, bf16[32,2,576]{2,1,0:T(2,128)(2,1)S(1)}, s32[32]{0:T(128)S(1)}, bf16[32,64,576]{2,1,0:T(8,128)(2,1)S(1)}) %tuple.47), branch_computations={%region_0.0_spmd, %region_1.0_spmd} | conditional | flops 2397440 | bytes 680380 | solution.py:160
  34.0 0.2 convolution_convert_fusion
  34.2 0.7 copy.22
  34.9 5.0 %all-to-all-start = ((bf16[32,2,576]{2,1,0:T(2,128)(2,1)}), bf16[32,2,576]{2,1,0:T(2,128)(2,1)S(1)}, u32[]{:S(2)}, u32[]{:S(2)}) async-start(bf16[32,2,576]{2,1,0:T(2,128)(2,1)} %copy.22), calls=%async_computation | async-start | bytes 163840 | tf_op jit(solution)/shard_map/cond/branch_1_fun/all_to_all | solution.py:143
  39.9 0.7 pick_cached.2
  40.6 6.7 %all-to-all-done = bf16[32,2,576]{2,1,0:T(2,128)(2,1)S(1)} async-done(((bf16[32,2,576]{2,1,0:T(2,128)(2,1)}), bf16[32,2,576]{2,1,0:T(2,128)(2,1)S(1)}, u32[]{:S(2)}, u32[]{:S(2)}) %all-to-all-start) | async-done | bytes 73760 | tf_op jit(solution)/shard_map/cond/branch_1_fun/all_to_all | solution.py:143
  47.3 0.1 reshape.17
  47.5 0.0 collective-permute-done.1
  47.5 8.8 %collective-permute-done = bf16[64,576]{1,0:T(8,128)(2,1)S(1)} collective-permute-done((bf16[64,576]{1,0:T(8,128)(2,1)}, bf16[64,576]{1,0:T(8,128)(2,1)S(1)}, u32[]{:S(2)}, u32[]{:S(2)}) %collective-permute-start) | collective-permute-done | bytes 73760 | tf_op jit(solution)/shard_map/ppermute | solution.py:159
  56.3 0.3 fusion.27
  56.7 0.2 fusion.19
  56.8 0.2 fusion.10
  57.1 0.9 pad_maximum_fusion
  58.0 4.8 %all-to-all-start.2 = ((bf16[32,4,576]{2,1,0:T(4,128)(2,1)}), bf16[32,4,576]{2,1,0:T(4,128)(2,1)S(1)}, u32[]{:S(2)}, u32[]{:S(2)}) async-start(bf16[32,4,576]{2,1,0:T(4,128)(2,1)} %pad_maximum_fusion), calls=%async_computation.2 | async-start | bytes 327680 | tf_op jit(solution)/shard_map/all_to_all | solution.py:176
  62.9 8.0 %all-to-all-done.2 = bf16[32,4,576]{2,1,0:T(4,128)(2,1)S(1)} async-done(((bf16[32,4,576]{2,1,0:T(4,128)(2,1)}), bf16[32,4,576]{2,1,0:T(4,128)(2,1)S(1)}, u32[]{:S(2)}, u32[]{:S(2)}) %all-to-all-start.2) | async-done | bytes 147488 | tf_op jit(solution)/shard_map/all_to_all | solution.py:176
  70.8 0.8 convolution_convert_fusion.2
  71.7 5.2 %project.1 = bf16[32,32,224]{2,1,0:T(8,128)(2,1)} custom-call(bf16[4,32,576]{2,1,0:T(8,128)(2,1)} %bitcast.13, bf16[2,512,128]{2,1,0:T(8,128)(2,1)} %up_ref.1, bf16[256,7168]{1,0:T(8,128)(2,1)} %out_proj_ref.1), custom_call_target="tpu_custom_call" | custom-call | flops 117440512 | bytes 3670016 | tf_op jit(solution)/shard_map/project/pallas_call | solution.py:104
  76.8 3.9 %all-to-all-start.3 = ((bf16[32,32,224]{2,1,0:T(8,128)(2,1)}), bf16[32,32,224]{2,1,0:T(8,128)(2,1)S(1)}, u32[]{:S(2)}, u32[]{:S(2)}) async-start(bf16[32,32,224]{2,1,0:T(8,128)(2,1)} %project.1), calls=%async_computation.3 | async-start | bytes 1048576 | tf_op jit(solution)/shard_map/all_to_all | solution.py:181
  80.8 0.7 copy.27
  81.5 11.0 %all-to-all-done.3 = bf16[32,32,224]{2,1,0:T(8,128)(2,1)S(1)} async-done(((bf16[32,32,224]{2,1,0:T(8,128)(2,1)}), bf16[32,32,224]{2,1,0:T(8,128)(2,1)S(1)}, u32[]{:S(2)}, u32[]{:S(2)}) %all-to-all-start.3) | async-done | bytes 458784 | tf_op jit(solution)/shard_map/all_to_all | solution.py:181
  92.4 0.7 reduce_sum.22
  (11 shorter events, 0.2 us)
Async XLA Ops:
  0.6 33.2 %copy-start.4 = (s32[32]{0:T(128)S(1)}, s32[32]{0:T(128)}, u32[]{:S(2)}) copy-start(s32[32]{0:T(128)} %constant.77.clone) | copy-start | bytes 388
  0.6 33.2 %copy-start.3 = (s32[32]{0:T(128)S(1)}, s32[32]{0:T(128)}, u32[]{:S(2)}) copy-start(s32[32]{0:T(128)} %param.14) | copy-start | bytes 388
  0.7 33.2 %copy-start = (bf16[32,64,576]{2,1,0:T(8,128)(2,1)S(1)}, bf16[32,64,576]{2,1,0:T(8,128)(2,1)}, u32[]{:S(2)}) copy-start(bf16[32,64,576]{2,1,0:T(8,128)(2,1)} %param.13) | copy-start | bytes 7077892
  0.7 33.2 %copy-start.2 = (bf16[32,2,576]{2,1,0:T(2,128)(2,1)S(1)}, bf16[32,2,576]{2,1,0:T(2,128)(2,1)}, u32[]{:S(2)}) copy-start(bf16[32,2,576]{2,1,0:T(2,128)(2,1)} %param.12) | copy-start | bytes 221188
  3.0 44.4 %collective-permute-start.1 = (bf16[64,576]{1,0:T(8,128)(2,1)}, bf16[64,576]{1,0:T(8,128)(2,1)S(1)}, u32[]{:S(2)}, u32[]{:S(2)}) collective-permute-start(bf16[64,576]{1,0:T(8,128)(2,1)} %pick_row.1), channel_id=1, source_target_pairs={{1,513},{2,34},{3,547},{4,68},{5,581},{6,102},{7,615},{8,136},{9,6... | collective-permute-start | bytes 221192 | tf_op jit(solution)/shard_map/ppermute | solution.py:161
  32.6 23.7 %collective-permute-start = (bf16[64,576]{1,0:T(8,128)(2,1)}, bf16[64,576]{1,0:T(8,128)(2,1)S(1)}, u32[]{:S(2)}, u32[]{:S(2)}) collective-permute-start(bf16[64,576]{1,0:T(8,128)(2,1)} %pick_row.1), channel_id=1, source_target_pairs={{0,0},{34,2},{36,36},{68,4},{70,38},{72,72},{102,6},{104,40},{106,... | collective-permute-start | bytes 221192 | tf_op jit(solution)/shard_map/ppermute | solution.py:159
  34.9 12.4 %all-to-all-start = ((bf16[32,2,576]{2,1,0:T(2,128)(2,1)}), bf16[32,2,576]{2,1,0:T(2,128)(2,1)S(1)}, u32[]{:S(2)}, u32[]{:S(2)}) async-start(bf16[32,2,576]{2,1,0:T(2,128)(2,1)} %copy.22), calls=%async_computation | async-start | bytes 163840 | tf_op jit(solution)/shard_map/cond/branch_1_fun/all_to_all | solution.py:143
  58.0 12.8 %all-to-all-start.2 = ((bf16[32,4,576]{2,1,0:T(4,128)(2,1)}), bf16[32,4,576]{2,1,0:T(4,128)(2,1)S(1)}, u32[]{:S(2)}, u32[]{:S(2)}) async-start(bf16[32,4,576]{2,1,0:T(4,128)(2,1)} %pad_maximum_fusion), calls=%async_computation.2 | async-start | bytes 327680 | tf_op jit(solution)/shard_map/all_to_all | solution.py:176
  71.7 9.1 %copy-start.1 = (bf16[32,4,576]{2,0,1:T(8,128)(2,1)S(1)}, bf16[32,4,576]{2,0,1:T(8,128)(2,1)}, u32[]{:S(2)}) copy-start(bf16[32,4,576]{2,0,1:T(8,128)(2,1)} %convolution_convert_fusion.2) | copy-start | bytes 442372
  76.8 15.6 %all-to-all-start.3 = ((bf16[32,32,224]{2,1,0:T(8,128)(2,1)}), bf16[32,32,224]{2,1,0:T(8,128)(2,1)S(1)}, u32[]{:S(2)}, u32[]{:S(2)}) async-start(bf16[32,32,224]{2,1,0:T(8,128)(2,1)} %project.1), calls=%async_computation.3 | async-start | bytes 1048576 | tf_op jit(solution)/shard_map/all_to_all | solution.py:181

commit v4 on v3

--- a/solution.py
+++ b/solution.py
@@ -9,19 +9,21 @@
 LAT = 512
 score_scale = 192.0 ** (-0.5)
 neg_fill = -1e30
+GRANT = 64_720_000
 VMEM = pl.BlockSpec(memory_space=pltpu.VMEM)
 SMEM = pl.BlockSpec(memory_space=pltpu.SMEM)
-ANY = pl.BlockSpec(memory_space=pl.ANY)
-
-
-def sigma(g):
-    return g // 2 + 16 * (g % 2)
+HBM = pl.BlockSpec(memory_space=pltpu.HBM)
+
+
+def sigma(g, n=32):
+    return (n // 4 + (g // 2 + n // 4) % (n // 2) + n // 2 * (g % 2)) % n
 
 
 def seat_request(n):
     d = lax.axis_index("ep")
     g = lax.axis_index("hd") * lax.axis_size("rep") + lax.axis_index("rep")
-    return lax.rem(lax.div(g, 2) + (n // 2) * lax.rem(g, 2) - d + n, n)
+    seat = n // 4 + lax.rem(lax.div(g, 2) + n // 4, n // 2) + (n // 2) * lax.rem(g, 2)
+    return lax.rem(seat - d + n, n)
 
 
 def leaving(z, n):
@@ -45,9 +47,10 @@
     return pl.pallas_call(
         pick_kernel,
         out_shape=jax.ShapeDtypeStruct(prefill_rows.shape[1:], prefill_rows.dtype),
-        in_specs=[SMEM, ANY],
+        in_specs=[SMEM, HBM],
         out_specs=VMEM,
         scratch_shapes=[pltpu.SemaphoreType.DMA],
+        compiler_params=pltpu.CompilerParams(vmem_limit_bytes=GRANT),
         name="pick_row",
     )(owner_rank, prefill_rows)
 
@@ -69,27 +72,37 @@
             jax.ShapeDtypeStruct(latent_cache.shape[1:], latent_cache.dtype),
             jax.ShapeDtypeStruct((8, positions), jnp.float32),
         ),
-        in_specs=[SMEM, ANY],
+        in_specs=[SMEM, HBM],
         out_specs=(VMEM, VMEM),
         scratch_shapes=[pltpu.SemaphoreType.DMA],
+        compiler_params=pltpu.CompilerParams(vmem_limit_bytes=GRANT),
         name="pick_cached",
     )(cached_lengths, latent_cache)
 
 
-def project_kernel(latent_ref, up_ref, out_proj_ref, parts_ref, weights, sems):
-    _, _, columns = parts_ref.shape
+def project_kernel(both_ref, up_ref, out_proj_ref, parts_ref, weights, sems):
+    n, _, columns = parts_ref.shape
     steps, _, wide = weights.shape
-    each = wide // columns
     copies = []
     for i in range(steps):
         window = out_proj_ref.at[:, pl.ds(i * wide, wide)]
         copies.append(pltpu.make_async_copy(window, weights.at[i], sems.at[i]))
         copies[i].start()
+    d = lax.axis_index("ep")
+    both = both_ref[...]
     heads = [
-        jnp.dot(latent_ref[i, :, :LAT], up_ref[i], preferred_element_type=jnp.float32)
+        jnp.dot(both[:, i, :LAT], up_ref[i], preferred_element_type=jnp.float32)
         for i in range(up_ref.shape[0])
     ]
     head_out = jnp.concatenate(heads, axis=1).astype(jnp.bfloat16)
+    seat = lax.broadcasted_iota(jnp.int32, (n, n), 1)
+    request = lax.broadcasted_iota(jnp.int32, (n, n), 0)
+    chip, core = lax.shift_right_logical(seat, 1), lax.bitwise_and(seat, 1)
+    seat = n // 4 + lax.bitwise_and(chip + n // 4, n // 2 - 1) + (n // 2) * core
+    choose = lax.bitwise_and(request + d - seat, n - 1) == 0
+    choose = jnp.where(choose, 1.0, 0.0).astype(jnp.bfloat16)
+    head_out = jnp.dot(choose, head_out, preferred_element_type=jnp.float32).astype(jnp.bfloat16)
+    each = wide // columns
     for i in range(steps):
         copies[i].wait()
         term = jnp.dot(head_out, weights[i], preferred_element_type=jnp.float32)
@@ -98,25 +111,24 @@
             parts_ref[each * i + k] = piece.astype(jnp.bfloat16)
 
 
-def project(latent, value_up, out_proj, n):
+def project(both, value_up, out_proj):
+    n = both.shape[0]
     depth, width = out_proj.shape
-    steps = n // 4
     return pl.pallas_call(
         project_kernel,
-        out_shape=jax.ShapeDtypeStruct((n, latent.shape[1], width // n), jnp.bfloat16),
-        in_specs=[VMEM, VMEM, ANY],
+        out_shape=jax.ShapeDtypeStruct((n, n, width // n), jnp.bfloat16),
+        in_specs=[VMEM, VMEM, HBM],
         out_specs=VMEM,
         scratch_shapes=[
-            pltpu.VMEM((steps, depth, width // steps), jnp.bfloat16),
-            pltpu.SemaphoreType.DMA((steps,)),
+            pltpu.VMEM((n // 4, depth, 4 * width // n), jnp.bfloat16),
+            pltpu.SemaphoreType.DMA((n // 4,)),
         ],
+        compiler_params=pltpu.CompilerParams(vmem_limit_bytes=GRANT),
         cost_estimate=pl.CostEstimate(
-            flops=2 * latent.shape[1] * depth * width,
-            bytes_accessed=2 * depth * width,
-            transcendentals=0,
+            flops=2 * n * depth * width, bytes_accessed=2 * depth * width, transcendentals=0
         ),
         name="project",
-    )(latent, value_up, out_proj)
+    )(both, value_up, out_proj)
 
 
 def body(queries, latent_cache, cached_lengths, prefill_rows, owner_rank, value_up, out_proj):
@@ -153,7 +165,7 @@
             jnp.zeros((8, positions), jnp.float32),
         )
 
-    early = (d <= 9 * n // 32) | (d >= 26 * n // 32)
+    early = (d < 12 * n // 32) | (d >= 28 * n // 32)
     row = pick_row(owner_rank, prefill_rows)
     operands = (queries, cached_lengths, latent_cache)
     late_row = lax.ppermute(row, ("ep", "hd", "rep"), later)
@@ -174,11 +186,10 @@
     latent = jnp.pad(latent, ((0, 0), (0, width - LAT)))
     both = jnp.concatenate([latent.reshape(n, 2, width), fresh_row.reshape(n, 2, width)], axis=1)
     both = lax.all_to_all(both, ("hd", "rep"), split_axis=0, concat_axis=0, tiled=True)
-    both = jnp.einsum("gr,ghk->rhk", choice(), both, preferred_element_type=jnp.float32)
-    both = both.astype(jnp.bfloat16)
-    fresh = both[:, 2:, :]
-    parts = project(jnp.moveaxis(both, 1, 0), value_up, out_proj, n)
+    parts = project(both, value_up, out_proj)
     arrived = lax.all_to_all(parts, ("hd", "rep"), split_axis=0, concat_axis=0, tiled=True)
+    fresh = jnp.einsum("gr,ghk->rhk", choice(), both[:, 2:, :], preferred_element_type=jnp.float32)
+    fresh = fresh.astype(jnp.bfloat16)
     mixed = arrived.astype(jnp.float32).sum(axis=0).astype(jnp.bfloat16)
     return (mixed, fresh)
 

time: 93.6 us -> 93 us (level)
  blocking collectives: 0 us -> 22.3 us
  waiting for transfers between devices: 34.5 us -> 16.7 us
  starting transfers between devices: 44.6 us -> 39.8 us
    ppermute x1, starting transfers between devices: 29.5 us -> 0.67 us  [body(): early_row = lax.ppermute(row, ('ep', 'hd', 'rep'), sooner)]
    all_to_all x1, starting transfers between devices: 5.03 us -> 33.7 us  [prepare(): lax.all_to_all(ordered.astype(jnp.bfloat16), ('hd', 'rep'), split_axis=0,...]
    all_to_all x0 -> x1, blocking collectives: none -> 22.3 us  [body(): lax.all_to_all(both, ('hd', 'rep'), split_axis=0, concat_axis=0, tiled=True)]
    ppermute x1, waiting for transfers between devices: 8.82 us -> 0.01 us  [body(): late_row = lax.ppermute(row, ('ep', 'hd', 'rep'), later)]
    all_to_all x1 -> x0, waiting for transfers between devices: 7.96 us -> none  [body(): lax.all_to_all(both, ('hd', 'rep'), split_axis=0, concat_axis=0, tiled=True)]
    all_to_all x1 -> x0, starting transfers between devices: 4.85 us -> none  [body(): lax.all_to_all(both, ('hd', 'rep'), split_axis=0, concat_axis=0, tiled=True)]
  transfers between devices with their start and end apart: 5 -> 4, of which waited for: 4 -> 2; matrix products, arithmetic and copies ran while one was open for 2% -> 2% of each run, Pallas kernels for 1% -> 2%
where the time goes in v4:
time: 93 us; the launch traced here: 92.3 us
  starting transfers between devices  39.8 us (43%)
  blocking collectives  22.3 us (24%)
  waiting for transfers between devices  16.7 us (18%)
  Pallas kernels  8.98 us (10%)
  local copies, waits for them, and re-layouts  1.68 us (2%)
  other arithmetic  1.11 us (1%)
    all_to_all x1, starting transfers between devices, prepare(): lax.all_to_all(ordered.astype(jnp.bfloat16), ('hd', 'rep'), split_axis=0,...  33.7 us
    all_to_all x1, blocking collectives, body(): lax.all_to_all(both, ('hd', 'rep'), split_axis=0, concat_axis=0, tiled=True)  22.3 us
    all_to_all x1, waiting for transfers between devices, body(): lax.all_to_all(parts, ('hd', 'rep'), split_axis=0, concat_axis=0, tiled=T...  10.7 us
    all_to_all x1, waiting for transfers between devices, prepare(): lax.all_to_all(ordered.astype(jnp.bfloat16), ('hd', 'rep'), split_axis=0,...  5.94 us
    pallas_call x1, Pallas kernels, project(): pl.pallas_call(project_kernel, out_shape=jax.ShapeDtypeStruct((n, n, widt...  5.15 us
    all_to_all x1, starting transfers between devices, body(): lax.all_to_all(parts, ('hd', 'rep'), split_axis=0, concat_axis=0, tiled=T...  3.91 us
    pallas_call x1, Pallas kernels, pick_row(): pl.pallas_call(pick_kernel, out_shape=jax.ShapeDtypeStruct(prefill_rows.s...  2.37 us
  transfers between devices with their start and end apart: 4, of which 2 were waited for; matrix products, arithmetic and copies ran while one was open for 2% of the time, Pallas kernels for 2%

profile of v4, /device:TPU:1, one launch (start us, length us, event | category | flops | bytes accessed | tf_op | source)
XLA Modules:
  0.0 92.3 jit_solution(13046102242832472074)
XLA Ops:
  0.6 0.0 copy-start.3
  0.6 0.0 copy-start.2
  0.7 0.0 copy-start.1
  0.7 2.4 %pick_row.1 = bf16[64,576]{1,0:T(8,128)(2,1)} custom-call(s32[32]{0:T(128)} %owner_ref.1, bf16[32,64,576]{2,1,0:T(8,128)(2,1)} %rows_ref.1), custom_call_target="tpu_custom_call" | custom-call | tf_op jit(solution)/shard_map/pick_row/pallas_call | solution.py:47
  3.0 0.7 collective-permute-start.1
  3.7 1.5 %collective-permute-start = (bf16[64,576]{1,0:T(8,128)(2,1)}, bf16[64,576]{1,0:T(8,128)(2,1)S(1)}, u32[]{:S(2)}, u32[]{:S(2)}) collective-permute-start(bf16[64,576]{1,0:T(8,128)(2,1)} %pick_row.1), channel_id=1, source_target_pairs={{1,1},{35,3},{37,37},{69,5},{71,39},{73,73},{103,7},{105,41},{107,... | collective-permute-start | bytes 221192 | tf_op jit(solution)/shard_map/ppermute | solution.py:171
  5.3 0.0 copy-done.3
  5.3 0.0 copy-done.2
  5.3 0.0 copy-done.1
  5.3 42.1 %conditional.2 = (bf16[64,576]{1,0:T(8,128)(2,1)S(1)}, bf16[64,576]{1,0:T(8,128)(2,1)S(1)}, f32[8,128]{1,0:T(8,128)S(1)}) conditional(s32[]{:T(128)} %convert_element_type.15, () %tuple.23, (s32[]{:T(128)}, s32[32]{0:T(128)S(1)}, bf16[32,2,576]{2,1,0:T(2,128)(2,1)S(1)}, s32[32]{0:T(128)S(1)}, bf16[32,64,576]{2,1,0:T(8,128)(2,1)}) %tuple.45), branch_computations={%region_0.0_spmd, %region_1.0_spmd} | conditional | flops 2397440 | bytes 680380 | solution.py:172
  5.3 0.2 convolution_convert_fusion
  5.5 0.7 copy.20
  6.2 33.7 %all-to-all-start = ((bf16[32,2,576]{2,1,0:T(2,128)(2,1)}), bf16[32,2,576]{2,1,0:T(2,128)(2,1)S(1)}, u32[]{:S(2)}, u32[]{:S(2)}) async-start(bf16[32,2,576]{2,1,0:T(2,128)(2,1)} %copy.20), calls=%async_computation | async-start | bytes 163840 | tf_op jit(solution)/shard_map/cond/branch_1_fun/all_to_all | solution.py:155
  39.9 1.5 %pick_cached.2 = (bf16[64,576]{1,0:T(8,128)(2,1)S(1)}, f32[8,128]{1,0:T(8,128)S(1)}) custom-call(s32[32]{0:T(128)S(1)} %get-tuple-element.29.lengths_ref, bf16[32,64,576]{2,1,0:T(8,128)(2,1)} %get-tuple-element.30.cache_ref), custom_call_target="tpu_custom_call" | custom-call | tf_op jit(solution)/shard_map/cond/branch_1_fun/pick_cached/pallas_call | solution.py:69
  41.4 5.9 %all-to-all-done = bf16[32,2,576]{2,1,0:T(2,128)(2,1)S(1)} async-done(((bf16[32,2,576]{2,1,0:T(2,128)(2,1)}), bf16[32,2,576]{2,1,0:T(2,128)(2,1)S(1)}, u32[]{:S(2)}, u32[]{:S(2)}) %all-to-all-start) | async-done | bytes 73760 | tf_op jit(solution)/shard_map/cond/branch_1_fun/all_to_all | solution.py:155
  47.3 0.1 reshape.17
  47.5 0.0 collective-permute-done.1
  47.5 0.0 collective-permute-done
  47.5 0.3 fusion.27
  47.8 0.2 fusion.19
  48.0 0.2 fusion.10
  48.3 0.2 pad_maximum_fusion
  48.5 22.3 %all_to_all.18.both_ref = bf16[32,4,576]{2,1,0:T(4,128)(2,1)} all-to-all(bf16[32,4,576]{2,1,0:T(4,128)(2,1)S(1)} %pad_maximum_fusion), channel_id=1, replica_groups=mesh['ep'=32,'hd'=4,'rep'=8] {'hd','rep'}, dimensions={0} | all-to-all | bytes 294912 | tf_op jit(solution)/shard_map/all_to_all | solution.py:188
  70.8 0.0 copy-start
  70.8 5.2 %project.1 = bf16[32,32,224]{2,1,0:T(8,128)(2,1)} custom-call(bf16[32,4,576]{2,1,0:T(4,128)(2,1)} %all_to_all.18.both_ref, bf16[2,512,128]{2,1,0:T(8,128)(2,1)} %up_ref.1, bf16[256,7168]{1,0:T(8,128)(2,1)} %out_proj_ref.1), custom_call_target="tpu_custom_call" | custom-call | flops 117440512 | bytes 3670016 | tf_op jit(solution)/shard_map/project/pallas_call | solution.py:117
  76.0 3.9 %all-to-all-start.3 = ((bf16[32,32,224]{2,1,0:T(8,128)(2,1)}), bf16[32,32,224]{2,1,0:T(8,128)(2,1)S(1)}, u32[]{:S(2)}, u32[]{:S(2)}) async-start(bf16[32,32,224]{2,1,0:T(8,128)(2,1)} %project.1), calls=%async_computation.3 | async-start | bytes 1048576 | tf_op jit(solution)/shard_map/all_to_all | solution.py:190
  79.9 0.0 copy-done
  79.9 0.1 slice.12
  80.0 0.1 convolution_convert_fusion.2
  80.2 0.7 copy.25
  80.9 10.7 %all-to-all-done.3 = bf16[32,32,224]{2,1,0:T(8,128)(2,1)S(1)} async-done(((bf16[32,32,224]{2,1,0:T(8,128)(2,1)}), bf16[32,32,224]{2,1,0:T(8,128)(2,1)S(1)}, u32[]{:S(2)}, u32[]{:S(2)}) %all-to-all-start.3) | async-done | bytes 458784 | tf_op jit(solution)/shard_map/all_to_all | solution.py:190
  91.6 0.7 reduce_sum.22
  (8 shorter events, 0.1 us)
Async XLA Ops:
  0.6 4.6 %copy-start.3 = (s32[32]{0:T(128)S(1)}, s32[32]{0:T(128)}, u32[]{:S(2)}) copy-start(s32[32]{0:T(128)} %constant.78.clone) | copy-start | bytes 388
  0.6 4.6 %copy-start.2 = (s32[32]{0:T(128)S(1)}, s32[32]{0:T(128)}, u32[]{:S(2)}) copy-start(s32[32]{0:T(128)} %param.14) | copy-start | bytes 388
  0.7 4.6 %copy-start.1 = (bf16[32,2,576]{2,1,0:T(2,128)(2,1)S(1)}, bf16[32,2,576]{2,1,0:T(2,128)(2,1)}, u32[]{:S(2)}) copy-start(bf16[32,2,576]{2,1,0:T(2,128)(2,1)} %param.12) | copy-start | bytes 221188
  3.0 44.4 %collective-permute-start.1 = (bf16[64,576]{1,0:T(8,128)(2,1)}, bf16[64,576]{1,0:T(8,128)(2,1)S(1)}, u32[]{:S(2)}, u32[]{:S(2)}) collective-permute-start(bf16[64,576]{1,0:T(8,128)(2,1)} %pick_row.1), channel_id=1, source_target_pairs={{0,512},{2,546},{3,35},{4,580},{5,69},{6,614},{7,103},{8,648},{9,1... | collective-permute-start | bytes 221192 | tf_op jit(solution)/shard_map/ppermute | solution.py:173
  3.7 43.8 %collective-permute-start = (bf16[64,576]{1,0:T(8,128)(2,1)}, bf16[64,576]{1,0:T(8,128)(2,1)S(1)}, u32[]{:S(2)}, u32[]{:S(2)}) collective-permute-start(bf16[64,576]{1,0:T(8,128)(2,1)} %pick_row.1), channel_id=1, source_target_pairs={{1,1},{35,3},{37,37},{69,5},{71,39},{73,73},{103,7},{105,41},{107,... | collective-permute-start | bytes 221192 | tf_op jit(solution)/shard_map/ppermute | solution.py:171
  6.2 41.1 %all-to-all-start = ((bf16[32,2,576]{2,1,0:T(2,128)(2,1)}), bf16[32,2,576]{2,1,0:T(2,128)(2,1)S(1)}, u32[]{:S(2)}, u32[]{:S(2)}) async-start(bf16[32,2,576]{2,1,0:T(2,128)(2,1)} %copy.20), calls=%async_computation | async-start | bytes 163840 | tf_op jit(solution)/shard_map/cond/branch_1_fun/all_to_all | solution.py:155
  70.8 9.1 %copy-start = (bf16[32,4,576]{2,1,0:T(4,128)(2,1)S(1)}, bf16[32,4,576]{2,1,0:T(4,128)(2,1)}, u32[]{:S(2)}) copy-start(bf16[32,4,576]{2,1,0:T(4,128)(2,1)} %all_to_all.18.both_ref) | copy-start | bytes 442372
  76.0 15.6 %all-to-all-start.3 = ((bf16[32,32,224]{2,1,0:T(8,128)(2,1)}), bf16[32,32,224]{2,1,0:T(8,128)(2,1)S(1)}, u32[]{:S(2)}, u32[]{:S(2)}) async-start(bf16[32,32,224]{2,1,0:T(8,128)(2,1)} %project.1), calls=%async_computation.3 | async-start | bytes 1048576 | tf_op jit(solution)/shard_map/all_to_all | solution.py:190

commit v5 on v4

--- a/solution.py
+++ b/solution.py
@@ -16,13 +16,13 @@
 
 
 def sigma(g, n=32):
-    return (n // 4 + (g // 2 + n // 4) % (n // 2) + n // 2 * (g % 2)) % n
+    return (n // 4 + g // 2 + n // 2 * (g % 2)) % n
 
 
 def seat_request(n):
     d = lax.axis_index("ep")
     g = lax.axis_index("hd") * lax.axis_size("rep") + lax.axis_index("rep")
-    seat = n // 4 + lax.rem(lax.div(g, 2) + n // 4, n // 2) + (n // 2) * lax.rem(g, 2)
+    seat = n // 4 + lax.div(g, 2) + (n // 2) * lax.rem(g, 2)
     return lax.rem(seat - d + n, n)
 
 
@@ -98,7 +98,7 @@
     seat = lax.broadcasted_iota(jnp.int32, (n, n), 1)
     request = lax.broadcasted_iota(jnp.int32, (n, n), 0)
     chip, core = lax.shift_right_logical(seat, 1), lax.bitwise_and(seat, 1)
-    seat = n // 4 + lax.bitwise_and(chip + n // 4, n // 2 - 1) + (n // 2) * core
+    seat = n // 4 + chip + (n // 2) * core
     choose = lax.bitwise_and(request + d - seat, n - 1) == 0
     choose = jnp.where(choose, 1.0, 0.0).astype(jnp.bfloat16)
     head_out = jnp.dot(choose, head_out, preferred_element_type=jnp.float32).astype(jnp.bfloat16)
@@ -123,7 +123,7 @@
             pltpu.VMEM((n // 4, depth, 4 * width // n), jnp.bfloat16),
             pltpu.SemaphoreType.DMA((n // 4,)),
         ],
-        compiler_params=pltpu.CompilerParams(vmem_limit_bytes=GRANT),
+        compiler_params=pltpu.CompilerParams(vmem_limit_bytes=63_600_000),
         cost_estimate=pl.CostEstimate(
             flops=2 * n * depth * width, bytes_accessed=2 * depth * width, transcendentals=0
         ),
@@ -165,7 +165,7 @@
             jnp.zeros((8, positions), jnp.float32),
         )
 
-    early = (d < 12 * n // 32) | (d >= 28 * n // 32)
+    early = d < n // 4
     row = pick_row(owner_rank, prefill_rows)
     operands = (queries, cached_lengths, latent_cache)
     late_row = lax.ppermute(row, ("ep", "hd", "rep"), later)

time: 93 us -> 95.5 us (1.027)
  the two profiles are of different devices: /device:TPU:1 before, /device:TPU:33 now
where the time goes in v5:
time: 95.5 us; the launch traced here: 95 us
  starting transfers between devices  41 us (43%)
  blocking collectives  23.7 us (25%)
  waiting for transfers between devices  16.7 us (17%)
  Pallas kernels  8.97 us (9%)
  local copies, waits for them, and re-layouts  1.68 us (2%)
  other arithmetic  1.11 us (1%)
    ppermute x1, starting transfers between devices, body(): early_row = lax.ppermute(row, ('ep', 'hd', 'rep'), sooner)  23.9 us
    all_to_all x1, blocking collectives, body(): lax.all_to_all(both, ('hd', 'rep'), split_axis=0, concat_axis=0, tiled=True)  23.7 us
    all_to_all x1, starting transfers between devices, prepare(): lax.all_to_all(ordered.astype(jnp.bfloat16), ('hd', 'rep'), split_axis=0,...  11.9 us
    all_to_all x1, waiting for transfers between devices, body(): lax.all_to_all(parts, ('hd', 'rep'), split_axis=0, concat_axis=0, tiled=T...  10.7 us
    all_to_all x1, waiting for transfers between devices, prepare(): lax.all_to_all(ordered.astype(jnp.bfloat16), ('hd', 'rep'), split_axis=0,...  5.95 us
    pallas_call x1, Pallas kernels, project(): pl.pallas_call(project_kernel, out_shape=jax.ShapeDtypeStruct((n, n, widt...  5.15 us
    all_to_all x1, starting transfers between devices, body(): lax.all_to_all(parts, ('hd', 'rep'), split_axis=0, concat_axis=0, tiled=T...  3.91 us
    pallas_call x1, Pallas kernels, pick_row(): pl.pallas_call(pick_kernel, out_shape=jax.ShapeDtypeStruct(prefill_rows.s...  2.37 us
  transfers between devices with their start and end apart: 4, of which 2 were waited for; matrix products, arithmetic and copies ran while one was open for 2% of the time, Pallas kernels for 2%

profile of v5, /device:TPU:33, one launch (start us, length us, event | category | flops | bytes accessed | tf_op | source)
XLA Modules:
  0.0 95.0 jit_solution(13187842631300673370)
XLA Ops:
  0.6 0.0 copy-start.3
  0.6 0.0 copy-start.2
  0.7 0.0 copy-start.1
  0.7 2.4 %pick_row.1 = bf16[64,576]{1,0:T(8,128)(2,1)} custom-call(s32[32]{0:T(128)} %owner_ref.1, bf16[32,64,576]{2,1,0:T(8,128)(2,1)} %rows_ref.1), custom_call_target="tpu_custom_call" | custom-call | tf_op jit(solution)/shard_map/pick_row/pallas_call | solution.py:47
  3.0 23.9 %collective-permute-start.1 = (bf16[64,576]{1,0:T(8,128)(2,1)}, bf16[64,576]{1,0:T(8,128)(2,1)S(1)}, u32[]{:S(2)}, u32[]{:S(2)}) collective-permute-start(bf16[64,576]{1,0:T(8,128)(2,1)} %pick_row.1), channel_id=1, source_target_pairs={{0,256},{1,769},{2,290},{3,803},{4,324},{5,837},{6,358},{7,871},{8... | collective-permute-start | bytes 221192 | tf_op jit(solution)/shard_map/ppermute | solution.py:173
  27.0 1.3 %collective-permute-start = (bf16[64,576]{1,0:T(8,128)(2,1)}, bf16[64,576]{1,0:T(8,128)(2,1)S(1)}, u32[]{:S(2)}, u32[]{:S(2)}) collective-permute-start(bf16[64,576]{1,0:T(8,128)(2,1)} %pick_row.1), channel_id=1, source_target_pairs={{17,17},{51,19},{53,53},{85,21},{87,55},{89,89},{119,23},{121,57},... | collective-permute-start | bytes 221192 | tf_op jit(solution)/shard_map/ppermute | solution.py:171
  28.3 0.0 copy-done.3
  28.3 0.0 copy-done.2
  28.3 0.0 copy-done.1
  28.3 20.4 %conditional.2 = (bf16[64,576]{1,0:T(8,128)(2,1)S(1)}, bf16[64,576]{1,0:T(8,128)(2,1)S(1)}, f32[8,128]{1,0:T(8,128)S(1)}) conditional(s32[]{:T(128)} %convert_element_type.15, () %tuple.23, (s32[]{:T(128)}, s32[32]{0:T(128)S(1)}, bf16[32,2,576]{2,1,0:T(2,128)(2,1)S(1)}, s32[32]{0:T(128)S(1)}, bf16[32,64,576]{2,1,0:T(8,128)(2,1)}) %tuple.45), branch_computations={%region_0.0_spmd, %region_1.0_spmd} | conditional | flops 2397440 | bytes 680380 | solution.py:172
  28.3 0.2 convolution_convert_fusion
  28.6 0.7 copy.20
  29.3 11.9 %all-to-all-start = ((bf16[32,2,576]{2,1,0:T(2,128)(2,1)}), bf16[32,2,576]{2,1,0:T(2,128)(2,1)S(1)}, u32[]{:S(2)}, u32[]{:S(2)}) async-start(bf16[32,2,576]{2,1,0:T(2,128)(2,1)} %copy.20), calls=%async_computation | async-start | bytes 163840 | tf_op jit(solution)/shard_map/cond/branch_1_fun/all_to_all | solution.py:155
  41.2 1.5 %pick_cached.2 = (bf16[64,576]{1,0:T(8,128)(2,1)S(1)}, f32[8,128]{1,0:T(8,128)S(1)}) custom-call(s32[32]{0:T(128)S(1)} %get-tuple-element.29.lengths_ref, bf16[32,64,576]{2,1,0:T(8,128)(2,1)} %get-tuple-element.30.cache_ref), custom_call_target="tpu_custom_call" | custom-call | tf_op jit(solution)/shard_map/cond/branch_1_fun/pick_cached/pallas_call | solution.py:69
  42.6 5.9 %all-to-all-done = bf16[32,2,576]{2,1,0:T(2,128)(2,1)S(1)} async-done(((bf16[32,2,576]{2,1,0:T(2,128)(2,1)}), bf16[32,2,576]{2,1,0:T(2,128)(2,1)S(1)}, u32[]{:S(2)}, u32[]{:S(2)}) %all-to-all-start) | async-done | bytes 73760 | tf_op jit(solution)/shard_map/cond/branch_1_fun/all_to_all | solution.py:155
  48.6 0.1 reshape.17
  48.7 0.0 collective-permute-done.1
  48.7 0.0 collective-permute-done
  48.8 0.3 fusion.27
  49.1 0.2 fusion.19
  49.3 0.2 fusion.10
  49.6 0.2 pad_maximum_fusion
  49.8 23.7 %all_to_all.18.both_ref = bf16[32,4,576]{2,1,0:T(4,128)(2,1)} all-to-all(bf16[32,4,576]{2,1,0:T(4,128)(2,1)S(1)} %pad_maximum_fusion), channel_id=1, replica_groups=mesh['ep'=32,'hd'=4,'rep'=8] {'hd','rep'}, dimensions={0} | all-to-all | bytes 294912 | tf_op jit(solution)/shard_map/all_to_all | solution.py:188
  73.5 0.0 copy-start
  73.5 5.2 %project.1 = bf16[32,32,224]{2,1,0:T(8,128)(2,1)} custom-call(bf16[32,4,576]{2,1,0:T(4,128)(2,1)} %all_to_all.18.both_ref, bf16[2,512,128]{2,1,0:T(8,128)(2,1)} %up_ref.1, bf16[256,7168]{1,0:T(8,128)(2,1)} %out_proj_ref.1), custom_call_target="tpu_custom_call" | custom-call | flops 117440512 | bytes 3670016 | tf_op jit(solution)/shard_map/project/pallas_call | solution.py:117
  78.7 3.9 %all-to-all-start.3 = ((bf16[32,32,224]{2,1,0:T(8,128)(2,1)}), bf16[32,32,224]{2,1,0:T(8,128)(2,1)S(1)}, u32[]{:S(2)}, u32[]{:S(2)}) async-start(bf16[32,32,224]{2,1,0:T(8,128)(2,1)} %project.1), calls=%async_computation.3 | async-start | bytes 1048576 | tf_op jit(solution)/shard_map/all_to_all | solution.py:190
  82.6 0.0 copy-done
  82.6 0.1 slice.12
  82.7 0.1 convolution_convert_fusion.2
  82.9 0.7 copy.25
  83.6 10.7 %all-to-all-done.3 = bf16[32,32,224]{2,1,0:T(8,128)(2,1)S(1)} async-done(((bf16[32,32,224]{2,1,0:T(8,128)(2,1)}), bf16[32,32,224]{2,1,0:T(8,128)(2,1)S(1)}, u32[]{:S(2)}, u32[]{:S(2)}) %all-to-all-start.3) | async-done | bytes 458784 | tf_op jit(solution)/shard_map/all_to_all | solution.py:190
  94.3 0.7 reduce_sum.22
  (8 shorter events, 0.1 us)
Async XLA Ops:
  0.6 27.6 %copy-start.3 = (s32[32]{0:T(128)S(1)}, s32[32]{0:T(128)}, u32[]{:S(2)}) copy-start(s32[32]{0:T(128)} %constant.73.clone) | copy-start | bytes 388
  0.6 27.6 %copy-start.2 = (s32[32]{0:T(128)S(1)}, s32[32]{0:T(128)}, u32[]{:S(2)}) copy-start(s32[32]{0:T(128)} %param.14) | copy-start | bytes 388
  0.7 27.6 %copy-start.1 = (bf16[32,2,576]{2,1,0:T(2,128)(2,1)S(1)}, bf16[32,2,576]{2,1,0:T(2,128)(2,1)}, u32[]{:S(2)}) copy-start(bf16[32,2,576]{2,1,0:T(2,128)(2,1)} %param.12) | copy-start | bytes 221188
  3.0 45.7 %collective-permute-start.1 = (bf16[64,576]{1,0:T(8,128)(2,1)}, bf16[64,576]{1,0:T(8,128)(2,1)S(1)}, u32[]{:S(2)}, u32[]{:S(2)}) collective-permute-start(bf16[64,576]{1,0:T(8,128)(2,1)} %pick_row.1), channel_id=1, source_target_pairs={{0,256},{1,769},{2,290},{3,803},{4,324},{5,837},{6,358},{7,871},{8... | collective-permute-start | bytes 221192 | tf_op jit(solution)/shard_map/ppermute | solution.py:173
  27.0 21.8 %collective-permute-start = (bf16[64,576]{1,0:T(8,128)(2,1)}, bf16[64,576]{1,0:T(8,128)(2,1)S(1)}, u32[]{:S(2)}, u32[]{:S(2)}) collective-permute-start(bf16[64,576]{1,0:T(8,128)(2,1)} %pick_row.1), channel_id=1, source_target_pairs={{17,17},{51,19},{53,53},{85,21},{87,55},{89,89},{119,23},{121,57},... | collective-permute-start | bytes 221192 | tf_op jit(solution)/shard_map/ppermute | solution.py:171
  29.3 19.3 %all-to-all-start = ((bf16[32,2,576]{2,1,0:T(2,128)(2,1)}), bf16[32,2,576]{2,1,0:T(2,128)(2,1)S(1)}, u32[]{:S(2)}, u32[]{:S(2)}) async-start(bf16[32,2,576]{2,1,0:T(2,128)(2,1)} %copy.20), calls=%async_computation | async-start | bytes 163840 | tf_op jit(solution)/shard_map/cond/branch_1_fun/all_to_all | solution.py:155
  73.5 9.1 %copy-start = (bf16[32,4,576]{2,1,0:T(4,128)(2,1)S(1)}, bf16[32,4,576]{2,1,0:T(4,128)(2,1)}, u32[]{:S(2)}) copy-start(bf16[32,4,576]{2,1,0:T(4,128)(2,1)} %all_to_all.18.both_ref) | copy-start | bytes 442372
  78.7 15.6 %all-to-all-start.3 = ((bf16[32,32,224]{2,1,0:T(8,128)(2,1)}), bf16[32,32,224]{2,1,0:T(8,128)(2,1)S(1)}, u32[]{:S(2)}, u32[]{:S(2)}) async-start(bf16[32,32,224]{2,1,0:T(8,128)(2,1)} %project.1), calls=%async_computation.3 | async-start | bytes 1048576 | tf_op jit(solution)/shard_map/all_to_all | solution.py:190

commit v6 on v5

--- a/solution.py
+++ b/solution.py
@@ -80,15 +80,23 @@
     )(cached_lengths, latent_cache)
 
 
-def project_kernel(both_ref, up_ref, out_proj_ref, parts_ref, weights, sems):
+def project_kernel(
+    both_hbm, up_hbm, out_proj_hbm, parts_hbm, both_ref, up_ref, weights, parts_ref, sems, out_sems
+):
     n, _, columns = parts_ref.shape
     steps, _, wide = weights.shape
-    copies = []
+    each = wide // columns
+    copies = [
+        pltpu.make_async_copy(both_hbm, both_ref, sems.at[steps]),
+        pltpu.make_async_copy(up_hbm, up_ref, sems.at[steps + 1]),
+    ]
     for i in range(steps):
-        window = out_proj_ref.at[:, pl.ds(i * wide, wide)]
+        window = out_proj_hbm.at[:, pl.ds(i * wide, wide)]
         copies.append(pltpu.make_async_copy(window, weights.at[i], sems.at[i]))
-        copies[i].start()
-    d = lax.axis_index("ep")
+    for copy in copies:
+        copy.start()
+    copies[0].wait()
+    copies[1].wait()
     both = both_ref[...]
     heads = [
         jnp.dot(both[:, i, :LAT], up_ref[i], preferred_element_type=jnp.float32)
@@ -99,31 +107,42 @@
     request = lax.broadcasted_iota(jnp.int32, (n, n), 0)
     chip, core = lax.shift_right_logical(seat, 1), lax.bitwise_and(seat, 1)
     seat = n // 4 + chip + (n // 2) * core
-    choose = lax.bitwise_and(request + d - seat, n - 1) == 0
+    choose = lax.bitwise_and(request + lax.axis_index("ep") - seat, n - 1) == 0
     choose = jnp.where(choose, 1.0, 0.0).astype(jnp.bfloat16)
     head_out = jnp.dot(choose, head_out, preferred_element_type=jnp.float32).astype(jnp.bfloat16)
-    each = wide // columns
+    sent = []
     for i in range(steps):
-        copies[i].wait()
+        copies[2 + i].wait()
         term = jnp.dot(head_out, weights[i], preferred_element_type=jnp.float32)
         for k in range(each):
             piece = term[:, k * columns : (k + 1) * columns]
             parts_ref[each * i + k] = piece.astype(jnp.bfloat16)
+        done = pl.ds(each * i, each)
+        sent.append(pltpu.make_async_copy(parts_ref.at[done], parts_hbm.at[done], out_sems.at[i]))
+        sent[i].start()
+    for copy in sent:
+        copy.wait()
 
 
 def project(both, value_up, out_proj):
     n = both.shape[0]
     depth, width = out_proj.shape
+    steps = 4
+    parts = jax.ShapeDtypeStruct((n, n, width // n), jnp.bfloat16)
     return pl.pallas_call(
         project_kernel,
-        out_shape=jax.ShapeDtypeStruct((n, n, width // n), jnp.bfloat16),
-        in_specs=[VMEM, VMEM, HBM],
-        out_specs=VMEM,
+        out_shape=parts,
+        in_specs=[HBM, HBM, HBM],
+        out_specs=HBM,
         scratch_shapes=[
-            pltpu.VMEM((n // 4, depth, 4 * width // n), jnp.bfloat16),
-            pltpu.SemaphoreType.DMA((n // 4,)),
+            pltpu.VMEM(both.shape, both.dtype),
+            pltpu.VMEM(value_up.shape, value_up.dtype),
+            pltpu.VMEM((steps, depth, width // steps), out_proj.dtype),
+            pltpu.VMEM(parts.shape, parts.dtype),
+            pltpu.SemaphoreType.DMA((steps + 2,)),
+            pltpu.SemaphoreType.DMA((steps,)),
         ],
-        compiler_params=pltpu.CompilerParams(vmem_limit_bytes=63_600_000),
+        compiler_params=pltpu.CompilerParams(vmem_limit_bytes=GRANT),
         cost_estimate=pl.CostEstimate(
             flops=2 * n * depth * width, bytes_accessed=2 * depth * width, transcendentals=0
         ),

time: 95.5 us -> 93.9 us (0.983)
  Pallas kernels: 8.97 us -> 7.43 us
    pallas_call x1, Pallas kernels: 5.15 us -> 3.61 us  [project(): pl.pallas_call(project_kernel, out_shape=parts, in_specs=[HBM, HBM, HBM],...]
where the time goes in v6:
time: 93.9 us; the launch traced here: 93.5 us
  starting transfers between devices  41 us (44%)
  blocking collectives  23.7 us (25%)
  waiting for transfers between devices  16.7 us (18%)
  Pallas kernels  7.43 us (8%)
  local copies, waits for them, and re-layouts  1.68 us (2%)
  other arithmetic  1.11 us (1%)
    ppermute x1, starting transfers between devices, body(): early_row = lax.ppermute(row, ('ep', 'hd', 'rep'), sooner)  23.9 us
    all_to_all x1, blocking collectives, body(): lax.all_to_all(both, ('hd', 'rep'), split_axis=0, concat_axis=0, tiled=True)  23.7 us
    all_to_all x1, starting transfers between devices, prepare(): lax.all_to_all(ordered.astype(jnp.bfloat16), ('hd', 'rep'), split_axis=0,...  11.9 us
    all_to_all x1, waiting for transfers between devices, body(): lax.all_to_all(parts, ('hd', 'rep'), split_axis=0, concat_axis=0, tiled=T...  10.7 us
    all_to_all x1, waiting for transfers between devices, prepare(): lax.all_to_all(ordered.astype(jnp.bfloat16), ('hd', 'rep'), split_axis=0,...  5.95 us
    all_to_all x1, starting transfers between devices, body(): lax.all_to_all(parts, ('hd', 'rep'), split_axis=0, concat_axis=0, tiled=T...  3.91 us
    pallas_call x1, Pallas kernels, project(): pl.pallas_call(project_kernel, out_shape=parts, in_specs=[HBM, HBM, HBM],...  3.61 us
    pallas_call x1, Pallas kernels, pick_row(): pl.pallas_call(pick_kernel, out_shape=jax.ShapeDtypeStruct(prefill_rows.s...  2.37 us
  transfers between devices with their start and end apart: 4, of which 2 were waited for; matrix products, arithmetic and copies ran while one was open for 2% of the time, Pallas kernels for 2%

profile of v6, /device:TPU:33, one launch (start us, length us, event | category | flops | bytes accessed | tf_op | source)
XLA Modules:
  0.0 93.5 jit_solution(10376314361342813669)
XLA Ops:
  0.6 0.0 copy-start.3
  0.6 0.0 copy-start.2
  0.7 0.0 copy-start.1
  0.7 2.4 %pick_row.1 = bf16[64,576]{1,0:T(8,128)(2,1)} custom-call(s32[32]{0:T(128)} %owner_ref.1, bf16[32,64,576]{2,1,0:T(8,128)(2,1)} %rows_ref.1), custom_call_target="tpu_custom_call" | custom-call | tf_op jit(solution)/shard_map/pick_row/pallas_call | solution.py:47
  3.0 23.9 %collective-permute-start.1 = (bf16[64,576]{1,0:T(8,128)(2,1)}, bf16[64,576]{1,0:T(8,128)(2,1)S(1)}, u32[]{:S(2)}, u32[]{:S(2)}) collective-permute-start(bf16[64,576]{1,0:T(8,128)(2,1)} %pick_row.1), channel_id=1, source_target_pairs={{0,256},{1,769},{2,290},{3,803},{4,324},{5,837},{6,358},{7,871},{8... | collective-permute-start | bytes 221192 | tf_op jit(solution)/shard_map/ppermute | solution.py:192
  27.0 1.3 %collective-permute-start = (bf16[64,576]{1,0:T(8,128)(2,1)}, bf16[64,576]{1,0:T(8,128)(2,1)S(1)}, u32[]{:S(2)}, u32[]{:S(2)}) collective-permute-start(bf16[64,576]{1,0:T(8,128)(2,1)} %pick_row.1), channel_id=1, source_target_pairs={{17,17},{51,19},{53,53},{85,21},{87,55},{89,89},{119,23},{121,57},... | collective-permute-start | bytes 221192 | tf_op jit(solution)/shard_map/ppermute | solution.py:190
  28.3 0.0 copy-done.3
  28.3 0.0 copy-done.2
  28.3 0.0 copy-done.1
  28.3 20.4 %conditional.2 = (bf16[64,576]{1,0:T(8,128)(2,1)S(1)}, bf16[64,576]{1,0:T(8,128)(2,1)S(1)}, f32[8,128]{1,0:T(8,128)S(1)}) conditional(s32[]{:T(128)} %convert_element_type.15, () %tuple.23, (s32[]{:T(128)}, s32[32]{0:T(128)S(1)}, bf16[32,2,576]{2,1,0:T(2,128)(2,1)S(1)}, s32[32]{0:T(128)S(1)}, bf16[32,64,576]{2,1,0:T(8,128)(2,1)}) %tuple.45), branch_computations={%region_0.0_spmd, %region_1.0_spmd} | conditional | flops 2397440 | bytes 680380 | solution.py:191
  28.3 0.2 convolution_convert_fusion
  28.6 0.7 copy.20
  29.3 11.9 %all-to-all-start = ((bf16[32,2,576]{2,1,0:T(2,128)(2,1)}), bf16[32,2,576]{2,1,0:T(2,128)(2,1)S(1)}, u32[]{:S(2)}, u32[]{:S(2)}) async-start(bf16[32,2,576]{2,1,0:T(2,128)(2,1)} %copy.20), calls=%async_computation | async-start | bytes 163840 | tf_op jit(solution)/shard_map/cond/branch_1_fun/all_to_all | solution.py:174
  41.2 1.5 %pick_cached.2 = (bf16[64,576]{1,0:T(8,128)(2,1)S(1)}, f32[8,128]{1,0:T(8,128)S(1)}) custom-call(s32[32]{0:T(128)S(1)} %get-tuple-element.29.lengths_ref, bf16[32,64,576]{2,1,0:T(8,128)(2,1)} %get-tuple-element.30.cache_ref), custom_call_target="tpu_custom_call" | custom-call | tf_op jit(solution)/shard_map/cond/branch_1_fun/pick_cached/pallas_call | solution.py:69
  42.6 5.9 %all-to-all-done = bf16[32,2,576]{2,1,0:T(2,128)(2,1)S(1)} async-done(((bf16[32,2,576]{2,1,0:T(2,128)(2,1)}), bf16[32,2,576]{2,1,0:T(2,128)(2,1)S(1)}, u32[]{:S(2)}, u32[]{:S(2)}) %all-to-all-start) | async-done | bytes 73760 | tf_op jit(solution)/shard_map/cond/branch_1_fun/all_to_all | solution.py:174
  48.6 0.1 reshape.17
  48.7 0.0 collective-permute-done.1
  48.7 0.0 collective-permute-done
  48.8 0.3 fusion.27
  49.1 0.2 fusion.19
  49.3 0.2 fusion.10
  49.6 0.2 pad_maximum_fusion
  49.8 23.7 %all_to_all.18.both_hbm = bf16[32,4,576]{2,1,0:T(4,128)(2,1)} all-to-all(bf16[32,4,576]{2,1,0:T(4,128)(2,1)S(1)} %pad_maximum_fusion), channel_id=1, replica_groups=mesh['ep'=32,'hd'=4,'rep'=8] {'hd','rep'}, dimensions={0} | all-to-all | bytes 294912 | tf_op jit(solution)/shard_map/all_to_all | solution.py:207
  73.5 0.0 copy-start
  73.5 3.6 %project.1 = bf16[32,32,224]{2,1,0:T(8,128)(2,1)} custom-call(bf16[32,4,576]{2,1,0:T(4,128)(2,1)} %all_to_all.18.both_hbm, bf16[2,512,128]{2,1,0:T(8,128)(2,1)} %up_hbm.1, bf16[256,7168]{1,0:T(8,128)(2,1)} %out_proj_hbm.1), custom_call_target="tpu_custom_call" | custom-call | flops 117440512 | bytes 3670016 | tf_op jit(solution)/shard_map/project/pallas_call | solution.py:132
  77.1 3.9 %all-to-all-start.3 = ((bf16[32,32,224]{2,1,0:T(8,128)(2,1)}), bf16[32,32,224]{2,1,0:T(8,128)(2,1)S(1)}, u32[]{:S(2)}, u32[]{:S(2)}) async-start(bf16[32,32,224]{2,1,0:T(8,128)(2,1)} %project.1), calls=%async_computation.3 | async-start | bytes 1048576 | tf_op jit(solution)/shard_map/all_to_all | solution.py:209
  81.1 0.0 copy-done
  81.1 0.1 slice.12
  81.2 0.1 convolution_convert_fusion.2
  81.3 0.7 copy.25
  82.0 10.7 %all-to-all-done.3 = bf16[32,32,224]{2,1,0:T(8,128)(2,1)S(1)} async-done(((bf16[32,32,224]{2,1,0:T(8,128)(2,1)}), bf16[32,32,224]{2,1,0:T(8,128)(2,1)S(1)}, u32[]{:S(2)}, u32[]{:S(2)}) %all-to-all-start.3) | async-done | bytes 458784 | tf_op jit(solution)/shard_map/all_to_all | solution.py:209
  92.8 0.7 reduce_sum.22
  (8 shorter events, 0.1 us)
Async XLA Ops:
  0.6 27.6 %copy-start.3 = (s32[32]{0:T(128)S(1)}, s32[32]{0:T(128)}, u32[]{:S(2)}) copy-start(s32[32]{0:T(128)} %constant.73.clone) | copy-start | bytes 388
  0.6 27.6 %copy-start.2 = (s32[32]{0:T(128)S(1)}, s32[32]{0:T(128)}, u32[]{:S(2)}) copy-start(s32[32]{0:T(128)} %param.14) | copy-start | bytes 388
  0.7 27.6 %copy-start.1 = (bf16[32,2,576]{2,1,0:T(2,128)(2,1)S(1)}, bf16[32,2,576]{2,1,0:T(2,128)(2,1)}, u32[]{:S(2)}) copy-start(bf16[32,2,576]{2,1,0:T(2,128)(2,1)} %param.12) | copy-start | bytes 221188
  3.0 45.7 %collective-permute-start.1 = (bf16[64,576]{1,0:T(8,128)(2,1)}, bf16[64,576]{1,0:T(8,128)(2,1)S(1)}, u32[]{:S(2)}, u32[]{:S(2)}) collective-permute-start(bf16[64,576]{1,0:T(8,128)(2,1)} %pick_row.1), channel_id=1, source_target_pairs={{0,256},{1,769},{2,290},{3,803},{4,324},{5,837},{6,358},{7,871},{8... | collective-permute-start | bytes 221192 | tf_op jit(solution)/shard_map/ppermute | solution.py:192
  27.0 21.8 %collective-permute-start = (bf16[64,576]{1,0:T(8,128)(2,1)}, bf16[64,576]{1,0:T(8,128)(2,1)S(1)}, u32[]{:S(2)}, u32[]{:S(2)}) collective-permute-start(bf16[64,576]{1,0:T(8,128)(2,1)} %pick_row.1), channel_id=1, source_target_pairs={{17,17},{51,19},{53,53},{85,21},{87,55},{89,89},{119,23},{121,57},... | collective-permute-start | bytes 221192 | tf_op jit(solution)/shard_map/ppermute | solution.py:190
  29.3 19.3 %all-to-all-start = ((bf16[32,2,576]{2,1,0:T(2,128)(2,1)}), bf16[32,2,576]{2,1,0:T(2,128)(2,1)S(1)}, u32[]{:S(2)}, u32[]{:S(2)}) async-start(bf16[32,2,576]{2,1,0:T(2,128)(2,1)} %copy.20), calls=%async_computation | async-start | bytes 163840 | tf_op jit(solution)/shard_map/cond/branch_1_fun/all_to_all | solution.py:174
  73.5 7.6 %copy-start = (bf16[32,4,576]{2,1,0:T(4,128)(2,1)S(1)}, bf16[32,4,576]{2,1,0:T(4,128)(2,1)}, u32[]{:S(2)}) copy-start(bf16[32,4,576]{2,1,0:T(4,128)(2,1)} %all_to_all.18.both_hbm) | copy-start | bytes 442372
  77.1 15.6 %all-to-all-start.3 = ((bf16[32,32,224]{2,1,0:T(8,128)(2,1)}), bf16[32,32,224]{2,1,0:T(8,128)(2,1)S(1)}, u32[]{:S(2)}, u32[]{:S(2)}) async-start(bf16[32,32,224]{2,1,0:T(8,128)(2,1)} %project.1), calls=%async_computation.3 | async-start | bytes 1048576 | tf_op jit(solution)/shard_map/all_to_all | solution.py:209

commit v7 on v6

--- a/solution.py
+++ b/solution.py
@@ -30,6 +30,10 @@
     half = n // 2
     rank = 12 * z * (z <= half) + (12 * half - 5 * (z - half)) * (z > half)
     return rank * n + z
+
+
+def comes_first(source, owner, n):
+    return (leaving(source, n) >= leaving(owner, n)) | ((source >= n // 4) & (owner >= n // 4))
 
 
 def pick_kernel(owner_ref, rows_ref, row_ref, sem):
@@ -161,8 +165,8 @@
         for k in range(n):
             owner = (sigma(k) - source) % n
             pair = (source * n + k, owner * n + k)
-            (later if leaving(source, n) >= leaving(owner, n) else sooner).append(pair)
-    from_later = leaving(mine, n) >= leaving(d, n)
+            (later if comes_first(source, owner, n) else sooner).append(pair)
+    from_later = comes_first(mine, d, n)
     seats = jnp.array([sigma(k) for k in range(n)], dtype=jnp.int32)
 
     def choice():

time: 93.9 us -> 93.1 us (level)
  the two profiles are of different devices: /device:TPU:33 before, /device:TPU:1 now
where the time goes in v7:
time: 93.1 us; the launch traced here: 91.7 us
  starting transfers between devices  41.9 us (45%)
  blocking collectives  21.1 us (23%)
  waiting for transfers between devices  16.7 us (18%)
  Pallas kernels  7.43 us (8%)
  local copies, waits for them, and re-layouts  1.68 us (2%)
  other arithmetic  1.11 us (1%)
    ppermute x1, starting transfers between devices, body(): early_row = lax.ppermute(row, ('ep', 'hd', 'rep'), sooner)  23.5 us
    all_to_all x1, blocking collectives, body(): lax.all_to_all(both, ('hd', 'rep'), split_axis=0, concat_axis=0, tiled=True)  21.1 us
    all_to_all x1, starting transfers between devices, prepare(): lax.all_to_all(ordered.astype(jnp.bfloat16), ('hd', 'rep'), split_axis=0,...  13.1 us
    all_to_all x1, waiting for transfers between devices, body(): lax.all_to_all(parts, ('hd', 'rep'), split_axis=0, concat_axis=0, tiled=T...  10.7 us
    all_to_all x1, waiting for transfers between devices, prepare(): lax.all_to_all(ordered.astype(jnp.bfloat16), ('hd', 'rep'), split_axis=0,...  5.95 us
    all_to_all x1, starting transfers between devices, body(): lax.all_to_all(parts, ('hd', 'rep'), split_axis=0, concat_axis=0, tiled=T...  3.91 us
    pallas_call x1, Pallas kernels, project(): pl.pallas_call(project_kernel, out_shape=parts, in_specs=[HBM, HBM, HBM],...  3.61 us
    pallas_call x1, Pallas kernels, pick_row(): pl.pallas_call(pick_kernel, out_shape=jax.ShapeDtypeStruct(prefill_rows.s...  2.37 us
  transfers between devices with their start and end apart: 4, of which 2 were waited for; matrix products, arithmetic and copies ran while one was open for 2% of the time, Pallas kernels for 2%

profile of v7, /device:TPU:1, one launch (start us, length us, event | category | flops | bytes accessed | tf_op | source)
XLA Modules:
  0.0 91.7 jit_solution(9170548204258360402)
XLA Ops:
  0.6 0.0 copy-start.3
  0.6 0.0 copy-start.2
  0.7 0.0 copy-start.1
  0.7 2.4 %pick_row.1 = bf16[64,576]{1,0:T(8,128)(2,1)} custom-call(s32[32]{0:T(128)} %owner_ref.1, bf16[32,64,576]{2,1,0:T(8,128)(2,1)} %rows_ref.1), custom_call_target="tpu_custom_call" | custom-call | tf_op jit(solution)/shard_map/pick_row/pallas_call | solution.py:51
  3.0 23.5 %collective-permute-start.1 = (bf16[64,576]{1,0:T(8,128)(2,1)}, bf16[64,576]{1,0:T(8,128)(2,1)S(1)}, u32[]{:S(2)}, u32[]{:S(2)}) collective-permute-start(bf16[64,576]{1,0:T(8,128)(2,1)} %pick_row.1), channel_id=1, source_target_pairs={{0,256},{1,769},{2,290},{3,803},{4,324},{5,837},{6,358},{7,871},{8... | collective-permute-start | bytes 221192 | tf_op jit(solution)/shard_map/ppermute | solution.py:196
  26.6 1.3 %collective-permute-start = (bf16[64,576]{1,0:T(8,128)(2,1)}, bf16[64,576]{1,0:T(8,128)(2,1)S(1)}, u32[]{:S(2)}, u32[]{:S(2)}) collective-permute-start(bf16[64,576]{1,0:T(8,128)(2,1)} %pick_row.1), channel_id=1, source_target_pairs={{17,17},{51,19},{53,53},{85,21},{87,55},{89,89},{119,23},{121,57},... | collective-permute-start | bytes 221192 | tf_op jit(solution)/shard_map/ppermute | solution.py:194
  27.9 0.0 copy-done.3
  27.9 0.0 copy-done.2
  27.9 0.0 copy-done.1
  27.9 21.6 %conditional.2 = (bf16[64,576]{1,0:T(8,128)(2,1)S(1)}, bf16[64,576]{1,0:T(8,128)(2,1)S(1)}, f32[8,128]{1,0:T(8,128)S(1)}) conditional(s32[]{:T(128)} %convert_element_type.15, () %tuple.23, (s32[]{:T(128)}, s32[32]{0:T(128)S(1)}, bf16[32,2,576]{2,1,0:T(2,128)(2,1)S(1)}, s32[32]{0:T(128)S(1)}, bf16[32,64,576]{2,1,0:T(8,128)(2,1)}) %tuple.45), branch_computations={%region_0.0_spmd, %region_1.0_spmd} | conditional | flops 2397440 | bytes 680380 | solution.py:195
  28.0 0.2 convolution_convert_fusion
  28.2 0.7 copy.20
  28.9 13.1 %all-to-all-start = ((bf16[32,2,576]{2,1,0:T(2,128)(2,1)}), bf16[32,2,576]{2,1,0:T(2,128)(2,1)S(1)}, u32[]{:S(2)}, u32[]{:S(2)}) async-start(bf16[32,2,576]{2,1,0:T(2,128)(2,1)} %copy.20), calls=%async_computation | async-start | bytes 163840 | tf_op jit(solution)/shard_map/cond/branch_1_fun/all_to_all | solution.py:178
  42.0 1.5 %pick_cached.2 = (bf16[64,576]{1,0:T(8,128)(2,1)S(1)}, f32[8,128]{1,0:T(8,128)S(1)}) custom-call(s32[32]{0:T(128)S(1)} %get-tuple-element.29.lengths_ref, bf16[32,64,576]{2,1,0:T(8,128)(2,1)} %get-tuple-element.30.cache_ref), custom_call_target="tpu_custom_call" | custom-call | tf_op jit(solution)/shard_map/cond/branch_1_fun/pick_cached/pallas_call | solution.py:73
  43.5 5.9 %all-to-all-done = bf16[32,2,576]{2,1,0:T(2,128)(2,1)S(1)} async-done(((bf16[32,2,576]{2,1,0:T(2,128)(2,1)}), bf16[32,2,576]{2,1,0:T(2,128)(2,1)S(1)}, u32[]{:S(2)}, u32[]{:S(2)}) %all-to-all-start) | async-done | bytes 73760 | tf_op jit(solution)/shard_map/cond/branch_1_fun/all_to_all | solution.py:178
  49.4 0.1 reshape.17
  49.6 0.0 collective-permute-done.1
  49.6 0.0 collective-permute-done
  49.7 0.3 fusion.27
  50.0 0.2 fusion.19
  50.2 0.2 fusion.10
  50.4 0.2 pad_maximum_fusion
  50.6 21.1 %all_to_all.18.both_hbm = bf16[32,4,576]{2,1,0:T(4,128)(2,1)} all-to-all(bf16[32,4,576]{2,1,0:T(4,128)(2,1)S(1)} %pad_maximum_fusion), channel_id=1, replica_groups=mesh['ep'=32,'hd'=4,'rep'=8] {'hd','rep'}, dimensions={0} | all-to-all | bytes 294912 | tf_op jit(solution)/shard_map/all_to_all | solution.py:211
  71.7 0.0 copy-start
  71.7 3.6 %project.1 = bf16[32,32,224]{2,1,0:T(8,128)(2,1)} custom-call(bf16[32,4,576]{2,1,0:T(4,128)(2,1)} %all_to_all.18.both_hbm, bf16[2,512,128]{2,1,0:T(8,128)(2,1)} %up_hbm.1, bf16[256,7168]{1,0:T(8,128)(2,1)} %out_proj_hbm.1), custom_call_target="tpu_custom_call" | custom-call | flops 117440512 | bytes 3670016 | tf_op jit(solution)/shard_map/project/pallas_call | solution.py:136
  75.4 3.9 %all-to-all-start.3 = ((bf16[32,32,224]{2,1,0:T(8,128)(2,1)}), bf16[32,32,224]{2,1,0:T(8,128)(2,1)S(1)}, u32[]{:S(2)}, u32[]{:S(2)}) async-start(bf16[32,32,224]{2,1,0:T(8,128)(2,1)} %project.1), calls=%async_computation.3 | async-start | bytes 1048576 | tf_op jit(solution)/shard_map/all_to_all | solution.py:213
  79.3 0.0 copy-done
  79.3 0.1 slice.12
  79.4 0.1 convolution_convert_fusion.2
  79.6 0.7 copy.25
  80.3 10.7 %all-to-all-done.3 = bf16[32,32,224]{2,1,0:T(8,128)(2,1)S(1)} async-done(((bf16[32,32,224]{2,1,0:T(8,128)(2,1)}), bf16[32,32,224]{2,1,0:T(8,128)(2,1)S(1)}, u32[]{:S(2)}, u32[]{:S(2)}) %all-to-all-start.3) | async-done | bytes 458784 | tf_op jit(solution)/shard_map/all_to_all | solution.py:213
  91.0 0.7 reduce_sum.22
  (8 shorter events, 0.1 us)
Async XLA Ops:
  0.6 27.3 %copy-start.3 = (s32[32]{0:T(128)S(1)}, s32[32]{0:T(128)}, u32[]{:S(2)}) copy-start(s32[32]{0:T(128)} %constant.73.clone) | copy-start | bytes 388
  0.6 27.3 %copy-start.2 = (s32[32]{0:T(128)S(1)}, s32[32]{0:T(128)}, u32[]{:S(2)}) copy-start(s32[32]{0:T(128)} %param.14) | copy-start | bytes 388
  0.7 27.3 %copy-start.1 = (bf16[32,2,576]{2,1,0:T(2,128)(2,1)S(1)}, bf16[32,2,576]{2,1,0:T(2,128)(2,1)}, u32[]{:S(2)}) copy-start(bf16[32,2,576]{2,1,0:T(2,128)(2,1)} %param.12) | copy-start | bytes 221188
  3.0 46.5 %collective-permute-start.1 = (bf16[64,576]{1,0:T(8,128)(2,1)}, bf16[64,576]{1,0:T(8,128)(2,1)S(1)}, u32[]{:S(2)}, u32[]{:S(2)}) collective-permute-start(bf16[64,576]{1,0:T(8,128)(2,1)} %pick_row.1), channel_id=1, source_target_pairs={{0,256},{1,769},{2,290},{3,803},{4,324},{5,837},{6,358},{7,871},{8... | collective-permute-start | bytes 221192 | tf_op jit(solution)/shard_map/ppermute | solution.py:196
  26.6 23.0 %collective-permute-start = (bf16[64,576]{1,0:T(8,128)(2,1)}, bf16[64,576]{1,0:T(8,128)(2,1)S(1)}, u32[]{:S(2)}, u32[]{:S(2)}) collective-permute-start(bf16[64,576]{1,0:T(8,128)(2,1)} %pick_row.1), channel_id=1, source_target_pairs={{17,17},{51,19},{53,53},{85,21},{87,55},{89,89},{119,23},{121,57},... | collective-permute-start | bytes 221192 | tf_op jit(solution)/shard_map/ppermute | solution.py:194
  28.9 20.5 %all-to-all-start = ((bf16[32,2,576]{2,1,0:T(2,128)(2,1)}), bf16[32,2,576]{2,1,0:T(2,128)(2,1)S(1)}, u32[]{:S(2)}, u32[]{:S(2)}) async-start(bf16[32,2,576]{2,1,0:T(2,128)(2,1)} %copy.20), calls=%async_computation | async-start | bytes 163840 | tf_op jit(solution)/shard_map/cond/branch_1_fun/all_to_all | solution.py:178
  71.7 7.6 %copy-start = (bf16[32,4,576]{2,1,0:T(4,128)(2,1)S(1)}, bf16[32,4,576]{2,1,0:T(4,128)(2,1)}, u32[]{:S(2)}) copy-start(bf16[32,4,576]{2,1,0:T(4,128)(2,1)} %all_to_all.18.both_hbm) | copy-start | bytes 442372
  75.4 15.6 %all-to-all-start.3 = ((bf16[32,32,224]{2,1,0:T(8,128)(2,1)}), bf16[32,32,224]{2,1,0:T(8,128)(2,1)S(1)}, u32[]{:S(2)}, u32[]{:S(2)}) async-start(bf16[32,32,224]{2,1,0:T(8,128)(2,1)} %project.1), calls=%async_computation.3 | async-start | bytes 1048576 | tf_op jit(solution)/shard_map/all_to_all | solution.py:213

commit v8 on v7

--- a/solution.py
+++ b/solution.py
@@ -16,13 +16,13 @@
 
 
 def sigma(g, n=32):
-    return (n // 4 + g // 2 + n // 2 * (g % 2)) % n
+    return (n // 4 + (g // 2 + n // 8) % (n // 2) + n // 2 * (g % 2)) % n
 
 
 def seat_request(n):
     d = lax.axis_index("ep")
     g = lax.axis_index("hd") * lax.axis_size("rep") + lax.axis_index("rep")
-    seat = n // 4 + lax.div(g, 2) + (n // 2) * lax.rem(g, 2)
+    seat = n // 4 + lax.rem(lax.div(g, 2) + n // 8, n // 2) + (n // 2) * lax.rem(g, 2)
     return lax.rem(seat - d + n, n)
 
 
@@ -33,7 +33,7 @@
 
 
 def comes_first(source, owner, n):
-    return (leaving(source, n) >= leaving(owner, n)) | ((source >= n // 4) & (owner >= n // 4))
+    return (leaving(source, n) >= leaving(owner, n)) & ((source < n // 4) | (owner < n // 4))
 
 
 def pick_kernel(owner_ref, rows_ref, row_ref, sem):
@@ -110,7 +110,7 @@
     seat = lax.broadcasted_iota(jnp.int32, (n, n), 1)
     request = lax.broadcasted_iota(jnp.int32, (n, n), 0)
     chip, core = lax.shift_right_logical(seat, 1), lax.bitwise_and(seat, 1)
-    seat = n // 4 + chip + (n // 2) * core
+    seat = n // 4 + lax.bitwise_and(chip + n // 8, n // 2 - 1) + (n // 2) * core
     choose = lax.bitwise_and(request + lax.axis_index("ep") - seat, n - 1) == 0
     choose = jnp.where(choose, 1.0, 0.0).astype(jnp.bfloat16)
     head_out = jnp.dot(choose, head_out, preferred_element_type=jnp.float32).astype(jnp.bfloat16)

time: 93.1 us -> 91.5 us (0.983)
  starting transfers between devices: 41.9 us -> 40.3 us
    ppermute x1, starting transfers between devices: 23.5 us -> 20.5 us  [body(): early_row = lax.ppermute(row, ('ep', 'hd', 'rep'), sooner)]
    all_to_all x1, starting transfers between devices: 13.1 us -> 14.6 us  [prepare(): lax.all_to_all(ordered.astype(jnp.bfloat16), ('hd', 'rep'), split_axis=0,...]
where the time goes in v8:
time: 91.5 us; the launch traced here: 90.2 us
  starting transfers between devices  40.3 us (44%)
  blocking collectives  21.1 us (23%)
  waiting for transfers between devices  16.7 us (18%)
  Pallas kernels  7.44 us (8%)
  local copies, waits for them, and re-layouts  1.68 us (2%)
  other arithmetic  1.11 us (1%)
    all_to_all x1, blocking collectives, body(): lax.all_to_all(both, ('hd', 'rep'), split_axis=0, concat_axis=0, tiled=True)  21.1 us
    ppermute x1, starting transfers between devices, body(): early_row = lax.ppermute(row, ('ep', 'hd', 'rep'), sooner)  20.5 us
    all_to_all x1, starting transfers between devices, prepare(): lax.all_to_all(ordered.astype(jnp.bfloat16), ('hd', 'rep'), split_axis=0,...  14.6 us
    all_to_all x1, waiting for transfers between devices, body(): lax.all_to_all(parts, ('hd', 'rep'), split_axis=0, concat_axis=0, tiled=T...  10.7 us
    all_to_all x1, waiting for transfers between devices, prepare(): lax.all_to_all(ordered.astype(jnp.bfloat16), ('hd', 'rep'), split_axis=0,...  5.94 us
    all_to_all x1, starting transfers between devices, body(): lax.all_to_all(parts, ('hd', 'rep'), split_axis=0, concat_axis=0, tiled=T...  3.92 us
    pallas_call x1, Pallas kernels, project(): pl.pallas_call(project_kernel, out_shape=parts, in_specs=[HBM, HBM, HBM],...  3.61 us
    pallas_call x1, Pallas kernels, pick_row(): pl.pallas_call(pick_kernel, out_shape=jax.ShapeDtypeStruct(prefill_rows.s...  2.37 us
  transfers between devices with their start and end apart: 4, of which 2 were waited for; matrix products, arithmetic and copies ran while one was open for 2% of the time, Pallas kernels for 2%

profile of v8, /device:TPU:1, one launch (start us, length us, event | category | flops | bytes accessed | tf_op | source)
XLA Modules:
  0.0 90.2 jit_solution(4222464355511220778)
XLA Ops:
  0.6 0.0 copy-start.3
  0.6 0.0 copy-start.2
  0.7 0.0 copy-start.1
  0.7 2.4 %pick_row.1 = bf16[64,576]{1,0:T(8,128)(2,1)} custom-call(s32[32]{0:T(128)} %owner_ref.1, bf16[32,64,576]{2,1,0:T(8,128)(2,1)} %rows_ref.1), custom_call_target="tpu_custom_call" | custom-call | tf_op jit(solution)/shard_map/pick_row/pallas_call | solution.py:51
  3.0 20.5 %collective-permute-start.1 = (bf16[64,576]{1,0:T(8,128)(2,1)}, bf16[64,576]{1,0:T(8,128)(2,1)S(1)}, u32[]{:S(2)}, u32[]{:S(2)}) collective-permute-start(bf16[64,576]{1,0:T(8,128)(2,1)} %pick_row.1), channel_id=1, source_target_pairs={{0,384},{1,897},{2,418},{3,931},{4,452},{5,965},{6,486},{7,999},{8... | collective-permute-start | bytes 221192 | tf_op jit(solution)/shard_map/ppermute | solution.py:196
  23.6 1.3 %collective-permute-start = (bf16[64,576]{1,0:T(8,128)(2,1)}, bf16[64,576]{1,0:T(8,128)(2,1)S(1)}, u32[]{:S(2)}, u32[]{:S(2)}) collective-permute-start(bf16[64,576]{1,0:T(8,128)(2,1)} %pick_row.1), channel_id=1, source_target_pairs={{9,9},{43,11},{45,45},{77,13},{79,47},{81,81},{111,15},{113,49},{1... | collective-permute-start | bytes 221192 | tf_op jit(solution)/shard_map/ppermute | solution.py:194
  24.9 0.0 copy-done.3
  24.9 0.0 copy-done.2
  24.9 0.0 copy-done.1
  24.9 23.0 %conditional.2 = (bf16[64,576]{1,0:T(8,128)(2,1)S(1)}, bf16[64,576]{1,0:T(8,128)(2,1)S(1)}, f32[8,128]{1,0:T(8,128)S(1)}) conditional(s32[]{:T(128)} %convert_element_type.15, () %tuple.23, (s32[]{:T(128)}, s32[32]{0:T(128)S(1)}, bf16[32,2,576]{2,1,0:T(2,128)(2,1)S(1)}, s32[32]{0:T(128)S(1)}, bf16[32,64,576]{2,1,0:T(8,128)(2,1)}) %tuple.45), branch_computations={%region_0.0_spmd, %region_1.0_spmd} | conditional | flops 2397440 | bytes 680380 | solution.py:195
  25.0 0.2 convolution_convert_fusion
  25.2 0.7 copy.20
  25.9 14.6 %all-to-all-start = ((bf16[32,2,576]{2,1,0:T(2,128)(2,1)}), bf16[32,2,576]{2,1,0:T(2,128)(2,1)S(1)}, u32[]{:S(2)}, u32[]{:S(2)}) async-start(bf16[32,2,576]{2,1,0:T(2,128)(2,1)} %copy.20), calls=%async_computation | async-start | bytes 163840 | tf_op jit(solution)/shard_map/cond/branch_1_fun/all_to_all | solution.py:178
  40.5 1.5 %pick_cached.2 = (bf16[64,576]{1,0:T(8,128)(2,1)S(1)}, f32[8,128]{1,0:T(8,128)S(1)}) custom-call(s32[32]{0:T(128)S(1)} %get-tuple-element.29.lengths_ref, bf16[32,64,576]{2,1,0:T(8,128)(2,1)} %get-tuple-element.30.cache_ref), custom_call_target="tpu_custom_call" | custom-call | tf_op jit(solution)/shard_map/cond/branch_1_fun/pick_cached/pallas_call | solution.py:73
  41.9 5.9 %all-to-all-done = bf16[32,2,576]{2,1,0:T(2,128)(2,1)S(1)} async-done(((bf16[32,2,576]{2,1,0:T(2,128)(2,1)}), bf16[32,2,576]{2,1,0:T(2,128)(2,1)S(1)}, u32[]{:S(2)}, u32[]{:S(2)}) %all-to-all-start) | async-done | bytes 73760 | tf_op jit(solution)/shard_map/cond/branch_1_fun/all_to_all | solution.py:178
  47.9 0.1 reshape.17
  48.0 0.0 collective-permute-done.1
  48.1 0.0 collective-permute-done
  48.1 0.3 fusion.27
  48.4 0.2 fusion.19
  48.6 0.2 fusion.10
  48.9 0.2 pad_maximum_fusion
  49.1 21.1 %all_to_all.18.both_hbm = bf16[32,4,576]{2,1,0:T(4,128)(2,1)} all-to-all(bf16[32,4,576]{2,1,0:T(4,128)(2,1)S(1)} %pad_maximum_fusion), channel_id=1, replica_groups=mesh['ep'=32,'hd'=4,'rep'=8] {'hd','rep'}, dimensions={0} | all-to-all | bytes 294912 | tf_op jit(solution)/shard_map/all_to_all | solution.py:211
  70.2 0.0 copy-start
  70.2 3.6 %project.1 = bf16[32,32,224]{2,1,0:T(8,128)(2,1)} custom-call(bf16[32,4,576]{2,1,0:T(4,128)(2,1)} %all_to_all.18.both_hbm, bf16[2,512,128]{2,1,0:T(8,128)(2,1)} %up_hbm.1, bf16[256,7168]{1,0:T(8,128)(2,1)} %out_proj_hbm.1), custom_call_target="tpu_custom_call" | custom-call | flops 117440512 | bytes 3670016 | tf_op jit(solution)/shard_map/project/pallas_call | solution.py:136
  73.8 3.9 %all-to-all-start.3 = ((bf16[32,32,224]{2,1,0:T(8,128)(2,1)}), bf16[32,32,224]{2,1,0:T(8,128)(2,1)S(1)}, u32[]{:S(2)}, u32[]{:S(2)}) async-start(bf16[32,32,224]{2,1,0:T(8,128)(2,1)} %project.1), calls=%async_computation.3 | async-start | bytes 1048576 | tf_op jit(solution)/shard_map/all_to_all | solution.py:213
  77.8 0.0 copy-done
  77.8 0.1 slice.12
  77.9 0.1 convolution_convert_fusion.2
  78.0 0.7 copy.25
  78.7 10.7 %all-to-all-done.3 = bf16[32,32,224]{2,1,0:T(8,128)(2,1)S(1)} async-done(((bf16[32,32,224]{2,1,0:T(8,128)(2,1)}), bf16[32,32,224]{2,1,0:T(8,128)(2,1)S(1)}, u32[]{:S(2)}, u32[]{:S(2)}) %all-to-all-start.3) | async-done | bytes 458784 | tf_op jit(solution)/shard_map/all_to_all | solution.py:213
  89.5 0.7 reduce_sum.22
  (8 shorter events, 0.1 us)
Async XLA Ops:
  0.6 24.3 %copy-start.3 = (s32[32]{0:T(128)S(1)}, s32[32]{0:T(128)}, u32[]{:S(2)}) copy-start(s32[32]{0:T(128)} %constant.78.clone) | copy-start | bytes 388
  0.6 24.3 %copy-start.2 = (s32[32]{0:T(128)S(1)}, s32[32]{0:T(128)}, u32[]{:S(2)}) copy-start(s32[32]{0:T(128)} %param.14) | copy-start | bytes 388
  0.7 24.3 %copy-start.1 = (bf16[32,2,576]{2,1,0:T(2,128)(2,1)S(1)}, bf16[32,2,576]{2,1,0:T(2,128)(2,1)}, u32[]{:S(2)}) copy-start(bf16[32,2,576]{2,1,0:T(2,128)(2,1)} %param.12) | copy-start | bytes 221188
  3.0 45.0 %collective-permute-start.1 = (bf16[64,576]{1,0:T(8,128)(2,1)}, bf16[64,576]{1,0:T(8,128)(2,1)S(1)}, u32[]{:S(2)}, u32[]{:S(2)}) collective-permute-start(bf16[64,576]{1,0:T(8,128)(2,1)} %pick_row.1), channel_id=1, source_target_pairs={{0,384},{1,897},{2,418},{3,931},{4,452},{5,965},{6,486},{7,999},{8... | collective-permute-start | bytes 221192 | tf_op jit(solution)/shard_map/ppermute | solution.py:196
  23.6 24.5 %collective-permute-start = (bf16[64,576]{1,0:T(8,128)(2,1)}, bf16[64,576]{1,0:T(8,128)(2,1)S(1)}, u32[]{:S(2)}, u32[]{:S(2)}) collective-permute-start(bf16[64,576]{1,0:T(8,128)(2,1)} %pick_row.1), channel_id=1, source_target_pairs={{9,9},{43,11},{45,45},{77,13},{79,47},{81,81},{111,15},{113,49},{1... | collective-permute-start | bytes 221192 | tf_op jit(solution)/shard_map/ppermute | solution.py:194
  25.9 22.0 %all-to-all-start = ((bf16[32,2,576]{2,1,0:T(2,128)(2,1)}), bf16[32,2,576]{2,1,0:T(2,128)(2,1)S(1)}, u32[]{:S(2)}, u32[]{:S(2)}) async-start(bf16[32,2,576]{2,1,0:T(2,128)(2,1)} %copy.20), calls=%async_computation | async-start | bytes 163840 | tf_op jit(solution)/shard_map/cond/branch_1_fun/all_to_all | solution.py:178
  70.2 7.6 %copy-start = (bf16[32,4,576]{2,1,0:T(4,128)(2,1)S(1)}, bf16[32,4,576]{2,1,0:T(4,128)(2,1)}, u32[]{:S(2)}) copy-start(bf16[32,4,576]{2,1,0:T(4,128)(2,1)} %all_to_all.18.both_hbm) | copy-start | bytes 442372
  73.8 15.6 %all-to-all-start.3 = ((bf16[32,32,224]{2,1,0:T(8,128)(2,1)}), bf16[32,32,224]{2,1,0:T(8,128)(2,1)S(1)}, u32[]{:S(2)}, u32[]{:S(2)}) async-start(bf16[32,32,224]{2,1,0:T(8,128)(2,1)} %project.1), calls=%async_computation.3 | async-start | bytes 1048576 | tf_op jit(solution)/shard_map/all_to_all | solution.py:213
